TPU v7x, 32 devices: a whole 2x2x4 slice. The times are simulated.
32 devices in a mesh: fsdp: 4 (over z), ctx: 2 (over x), tp: 4 (over y, core).
Axes of the slice: x: 2, y: 2, z: 4, core: 2. Of those that a mesh axis runs over, the one named last changes fastest.
Arguments:
- tokens: bfloat16 [8, 2048, 1024], P('fsdp', ('ctx', 'tp')), may hold values from -6 to 6
- cotangent: bfloat16 [8, 2048, 1024], P('fsdp', ('ctx', 'tp')), may hold values from -6 to 6
- lengths: int32 [8, 2], P('fsdp'), may hold values from 1 to 1536, 1792 in all within a row
- deal: int32 [8, 2048], P('fsdp'), may hold values from 0 to 2047, as said below
- ln1_gain: bfloat16 [1024], P('fsdp'), may hold values from 0.5 to 1.5
- ln1_bias: bfloat16 [1024], P('fsdp'), may hold values from -1.25 to 1.25
- w_qkv: bfloat16 [1024, 3, 1024], P('fsdp', None, 'tp'), may hold values from -0.1875 to 0.1875
- b_qv: bfloat16 [2, 16, 64], P(None, 'tp', 'fsdp'), may hold values from -3 to 3
- w_out: bfloat16 [1024, 1024], P('tp', 'fsdp'), may hold values from -1.5 to 1.5
- b_out: bfloat16 [1024], P('fsdp'), may hold values from -1.25 to 1.25
- ln2_gain: bfloat16 [1024], P('fsdp'), may hold values from 0.5 to 1.5
- ln2_bias: bfloat16 [1024], P('fsdp'), may hold values from -1.25 to 1.25
- w_fc: bfloat16 [1024, 4096], P('fsdp', 'tp'), may hold values from -0.1875 to 0.1875
- b_fc: bfloat16 [64, 64], P('tp', 'fsdp'), may hold values from -1.25 to 1.25
- w_proj: bfloat16 [4096, 1024], P('tp', 'fsdp'), may hold values from -0.125 to 0.125
- b_proj: bfloat16 [1024], P('fsdp'), may hold values from -1.25 to 1.25
Outputs:
- layer_out: bfloat16 [8, 2048, 1024], P('fsdp', ('ctx', 'tp'))
- grad_tokens: float32 [8, 2048, 1024], P('fsdp', ('ctx', 'tp'))
- grad_ln1_gain: float32 [1024], P('fsdp')
- grad_ln1_bias: float32 [1024], P('fsdp')
- grad_w_qkv: float32 [1024, 3, 1024], P('fsdp', None, 'tp')
- grad_b_qv: float32 [2, 16, 64], P(None, 'tp', 'fsdp')
- grad_w_out: float32 [1024, 1024], P('tp', 'fsdp')
- grad_b_out: float32 [1024], P('fsdp')
- grad_ln2_gain: float32 [1024], P('fsdp')
- grad_ln2_bias: float32 [1024], P('fsdp')
- grad_w_fc: float32 [1024, 4096], P('fsdp', 'tp')
- grad_b_fc: float32 [64, 64], P('tp', 'fsdp')
- grad_w_proj: float32 [4096, 1024], P('tp', 'fsdp')
- grad_b_proj: float32 [1024], P('fsdp')
Inputs may be any that keep to these rules, and one draw needn't show every extreme that they name: Each row lists the lengths of its 2 sequences in order; they sum to 1792, the rest of the row being padding. `deal`: each row is a permutation of 0 to 2047 that moves aligned blocks of 64 positions whole.
All inputs are finite; a program needn't handle non-finite values.
Results may differ from a plain program's by a relative error of at most 0.019.
Values may be sent and summed in bfloat16 or wider, within the bound.
No kernel may reach another device: no remote copies, remote signals or barrier semaphores. Data moves between devices by JAX's collectives and lax.ppermute only.
A program may use at most 320 MiB of HBM per device.

v0:
```python
import jax
import jax.numpy as jnp
from jax import lax
from jax.sharding import PartitionSpec as P

EPSILON = 1e-05
NEGATIVE = -1e30
GELU_SCALE = 0.7978845608028654
GELU_CUBIC = 0.044715


def layer_norm(source, gain_vec, bias_vec):
    center = jnp.mean(source, axis=-1, keepdims=True)
    offsets = source - center
    spread = jnp.mean(offsets * offsets, axis=-1, keepdims=True)
    return offsets * lax.rsqrt(spread + EPSILON) * gain_vec + bias_vec


def gelu_tanh(source):
    return (
        0.5
        * source
        * (1.0 + jnp.tanh(GELU_SCALE * (source + GELU_CUBIC * source * source * source)))
    )


def shards(
    tokens,
    cotangent,
    lengths,
    deal,
    ln1_gain,
    ln1_bias,
    w_qkv,
    b_qv,
    w_out,
    b_out,
    ln2_gain,
    ln2_bias,
    w_fc,
    b_fc,
    w_proj,
    b_proj,
):
    micro_count, share_len, model_width = tokens.shape
    row_len = deal.shape[1]
    seq_count = lengths.shape[1]
    query_len = row_len // lax.axis_size("ctx")
    query_start = lax.axis_index("ctx") * query_len
    own_start = query_start + lax.axis_index("tp") * share_len
    f32 = jnp.float32
    bf16 = jnp.bfloat16
    layer_rows = []
    input_rows = []
    running = None
    for micro_index in range(micro_count):
        gain_one = lax.all_gather(ln1_gain, "fsdp", axis=0, tiled=True)
        bias_one = lax.all_gather(ln1_bias, "fsdp", axis=0, tiled=True)
        qkv_weight = lax.all_gather(w_qkv, "fsdp", axis=0, tiled=True)
        qv_bias = lax.all_gather(b_qv, "fsdp", axis=2, tiled=True)
        out_weight = lax.all_gather(w_out, "fsdp", axis=1, tiled=True)
        out_bias = lax.all_gather(b_out, "fsdp", axis=0, tiled=True)
        gain_two = lax.all_gather(ln2_gain, "fsdp", axis=0, tiled=True)
        bias_two = lax.all_gather(ln2_bias, "fsdp", axis=0, tiled=True)
        fc_weight = lax.all_gather(w_fc, "fsdp", axis=0, tiled=True)
        fc_bias = lax.all_gather(b_fc, "fsdp", axis=1, tiled=True)
        proj_weight = lax.all_gather(w_proj, "fsdp", axis=1, tiled=True)
        proj_bias = lax.all_gather(b_proj, "fsdp", axis=0, tiled=True)
        local_width = qkv_weight.shape[2]
        local_heads = qv_bias.shape[1]
        head_size = qv_bias.shape[2]
        scaling = head_size ** (-0.5)
        qkv_flat = qkv_weight.reshape(model_width, 3 * local_width)
        positions = deal[micro_index]
        seq_ends = jnp.cumsum(lengths[micro_index])
        segment = jnp.sum((positions[:, None] >= seq_ends[None, :]).astype(jnp.int32), axis=1)
        query_pos = lax.dynamic_slice_in_dim(positions, query_start, query_len)
        query_seg = lax.dynamic_slice_in_dim(segment, query_start, query_len)
        allowed = (query_seg[:, None] == segment[None, :]) & (
            positions[None, :] <= query_pos[:, None]
        )
        own_valid = (lax.dynamic_slice_in_dim(segment, own_start, share_len) < seq_count).astype(
            f32
        )
        source = tokens[micro_index].astype(f32)
        normed_one, pull_one = jax.vjp(
            layer_norm, source, gain_one.astype(f32), bias_one.astype(f32)
        )
        gathered_one = lax.all_gather(normed_one.astype(bf16), "tp", axis=0, tiled=True)
        projected = jnp.dot(gathered_one, qkv_flat, preferred_element_type=f32)
        head_bias = qv_bias.reshape(2, local_width).astype(f32)
        query_low = (projected[:, :local_width] + head_bias[0]).astype(bf16)
        keys_own = projected[:, local_width : 2 * local_width].astype(bf16)
        values_own = (projected[:, 2 * local_width :] + head_bias[1]).astype(bf16)
        keys_all = lax.all_gather(keys_own, "ctx", axis=0, tiled=True)
        values_all = lax.all_gather(values_own, "ctx", axis=0, tiled=True)
        query_heads = query_low.reshape(query_len, local_heads, head_size)
        key_heads = keys_all.reshape(row_len, local_heads, head_size)
        value_heads = values_all.reshape(row_len, local_heads, head_size)

        def score_block():
            raw_scores = (
                jnp.einsum("qhd,khd->hqk", query_heads, key_heads, preferred_element_type=f32)
                * scaling
            )
            return jnp.where(allowed[None], raw_scores, NEGATIVE)

        scores = score_block()
        row_top = jnp.max(scores, axis=-1, keepdims=True)
        row_total = jnp.sum(jnp.exp(scores - row_top), axis=-1, keepdims=True)
        log_total = row_top + jnp.log(row_total)
        attention = jnp.exp(scores - log_total)
        mixed_low = (
            jnp.einsum(
                "hqk,khd->qhd", attention.astype(bf16), value_heads, preferred_element_type=f32
            )
            .reshape(query_len, local_width)
            .astype(bf16)
        )
        mixer_part = jnp.dot(mixed_low, out_weight, preferred_element_type=f32)
        hidden_one = (
            source
            + lax.psum_scatter(mixer_part, "tp", scatter_dimension=0, tiled=True)
            + out_bias.astype(f32)
        )
        normed_two, pull_two = jax.vjp(
            layer_norm, hidden_one, gain_two.astype(f32), bias_two.astype(f32)
        )
        gathered_two = lax.all_gather(normed_two.astype(bf16), "tp", axis=0, tiled=True)
        before = jnp.dot(gathered_two, fc_weight, preferred_element_type=f32) + fc_bias.reshape(
            -1
        ).astype(f32)
        activated, pull_gelu = jax.vjp(gelu_tanh, before)
        act_low = activated.astype(bf16)
        feed_part = jnp.dot(act_low, proj_weight, preferred_element_type=f32)
        layer_out = (
            hidden_one
            + lax.psum_scatter(
                feed_part.astype(jnp.bfloat16), "tp", scatter_dimension=0, tiled=True
            ).astype(jnp.float32)
            + proj_bias.astype(f32)
        )
        out_grad = cotangent[micro_index].astype(f32) * own_valid[:, None]
        grad_proj_bias = jnp.sum(out_grad, axis=0)
        gathered_grad = lax.all_gather(out_grad.astype(bf16), "tp", axis=0, tiled=True)
        grad_proj = jnp.einsum("tf,td->fd", act_low, gathered_grad, preferred_element_type=f32)
        (before_grad,) = pull_gelu(
            jnp.einsum("td,fd->tf", gathered_grad, proj_weight, preferred_element_type=f32)
        )
        before_low = before_grad.astype(bf16)
        grad_fc_bias = jnp.sum(before_low.astype(f32), axis=0).reshape(fc_bias.shape)
        grad_fc = jnp.einsum("td,tf->df", gathered_two, before_low, preferred_element_type=f32)
        second_part = jnp.einsum("tf,df->td", before_low, fc_weight, preferred_element_type=f32)
        second_norm_grad = lax.psum_scatter(
            second_part.astype(jnp.bfloat16), "tp", scatter_dimension=0, tiled=True
        ).astype(jnp.float32)
        hidden_back, grad_gain_two, grad_bias_two = pull_two(second_norm_grad)
        hidden_grad = out_grad + hidden_back
        grad_out_bias = jnp.sum(hidden_grad, axis=0)
        residual_all = lax.all_gather(hidden_grad.astype(bf16), "tp", axis=0, tiled=True)
        grad_out_w = jnp.einsum("tc,td->cd", mixed_low, residual_all, preferred_element_type=f32)
        mixed_grad = (
            jnp.einsum("td,cd->tc", residual_all, out_weight, preferred_element_type=f32)
            .astype(bf16)
            .reshape(query_len, local_heads, head_size)
        )
        attention = jnp.exp(score_block() - log_total)
        value_grad = jnp.einsum(
            "hqk,qhd->khd", attention.astype(bf16), mixed_grad, preferred_element_type=f32
        )
        attention_grad = jnp.einsum(
            "qhd,khd->hqk", mixed_grad, value_heads, preferred_element_type=f32
        )
        row_delta = jnp.sum(attention * attention_grad, axis=-1, keepdims=True)
        score_grad = (attention * (attention_grad - row_delta)).astype(bf16)
        query_grad = (
            jnp.einsum("hqk,khd->qhd", score_grad, key_heads, preferred_element_type=f32) * scaling
        )
        key_grad = (
            jnp.einsum("hqk,qhd->khd", score_grad, query_heads, preferred_element_type=f32)
            * scaling
        )
        key_own_grad = lax.psum_scatter(
            key_grad.reshape(row_len, local_width).astype(jnp.bfloat16),
            "ctx",
            scatter_dimension=0,
            tiled=True,
        ).astype(jnp.float32)
        value_own_grad = lax.psum_scatter(
            value_grad.reshape(row_len, local_width).astype(jnp.bfloat16),
            "ctx",
            scatter_dimension=0,
            tiled=True,
        ).astype(jnp.float32)
        proj_grad = jnp.concatenate(
            [query_grad.reshape(query_len, local_width), key_own_grad, value_own_grad], axis=1
        ).astype(bf16)
        grad_qv_bias = jnp.stack(
            [
                jnp.sum(proj_grad[:, :local_width].astype(f32), axis=0),
                jnp.sum(proj_grad[:, 2 * local_width :].astype(f32), axis=0),
            ]
        ).reshape(qv_bias.shape)
        grad_qkv = jnp.einsum(
            "td,tc->dc", gathered_one, proj_grad, preferred_element_type=f32
        ).reshape(qkv_weight.shape)
        first_part = jnp.einsum("tc,dc->td", proj_grad, qkv_flat, preferred_element_type=f32)
        first_norm_grad = lax.psum_scatter(
            first_part.astype(jnp.bfloat16), "tp", scatter_dimension=0, tiled=True
        ).astype(jnp.float32)
        source_grad, grad_gain_one, grad_bias_one = pull_one(first_norm_grad)
        grad_set = (
            grad_gain_one,
            grad_bias_one,
            grad_qkv,
            grad_qv_bias,
            grad_out_w,
            grad_out_bias,
            grad_gain_two,
            grad_bias_two,
            grad_fc,
            grad_fc_bias,
            grad_proj,
            grad_proj_bias,
        )
        layer_row, input_row, grad_set = (
            layer_out.astype(bf16),
            hidden_grad + source_grad,
            grad_set,
        )
        layer_rows.append(layer_row)
        input_rows.append(input_row)
        grad_set = (
            lax.psum_scatter(
                grad_set[0].astype(jnp.bfloat16), "fsdp", scatter_dimension=0, tiled=True
            ).astype(jnp.float32),
            lax.psum_scatter(
                grad_set[1].astype(jnp.bfloat16), "fsdp", scatter_dimension=0, tiled=True
            ).astype(jnp.float32),
            lax.psum_scatter(
                grad_set[2].astype(jnp.bfloat16), "fsdp", scatter_dimension=0, tiled=True
            ).astype(jnp.float32),
            lax.psum_scatter(
                grad_set[3].astype(jnp.bfloat16), "fsdp", scatter_dimension=2, tiled=True
            ).astype(jnp.float32),
            lax.psum_scatter(
                grad_set[4].astype(jnp.bfloat16), "fsdp", scatter_dimension=1, tiled=True
            ).astype(jnp.float32),
            lax.psum_scatter(
                grad_set[5].astype(jnp.bfloat16), "fsdp", scatter_dimension=0, tiled=True
            ).astype(jnp.float32),
            lax.psum_scatter(
                grad_set[6].astype(jnp.bfloat16), "fsdp", scatter_dimension=0, tiled=True
            ).astype(jnp.float32),
            lax.psum_scatter(
                grad_set[7].astype(jnp.bfloat16), "fsdp", scatter_dimension=0, tiled=True
            ).astype(jnp.float32),
            lax.psum_scatter(
                grad_set[8].astype(jnp.bfloat16), "fsdp", scatter_dimension=0, tiled=True
            ).astype(jnp.float32),
            lax.psum_scatter(
                grad_set[9].astype(jnp.bfloat16), "fsdp", scatter_dimension=1, tiled=True
            ).astype(jnp.float32),
            lax.psum_scatter(
                grad_set[10].astype(jnp.bfloat16), "fsdp", scatter_dimension=1, tiled=True
            ).astype(jnp.float32),
            lax.psum_scatter(
                grad_set[11].astype(jnp.bfloat16), "fsdp", scatter_dimension=0, tiled=True
            ).astype(jnp.float32),
        )
        running = grad_set if running is None else jax.tree.map(jnp.add, running, grad_set)
    matrix_part = (
        lax.psum(running[2].astype(jnp.bfloat16), "ctx").astype(jnp.float32),
        lax.psum(running[3].astype(jnp.bfloat16), "ctx").astype(jnp.float32),
        lax.psum(running[4].astype(jnp.bfloat16), "ctx").astype(jnp.float32),
        lax.psum(running[8].astype(jnp.bfloat16), "ctx").astype(jnp.float32),
        lax.psum(running[9].astype(jnp.bfloat16), "ctx").astype(jnp.float32),
        lax.psum(running[10].astype(jnp.bfloat16), "ctx").astype(jnp.float32),
    )
    vector_part = lax.psum(
        (running[0], running[1], running[5], running[6], running[7], running[11]), ("ctx", "tp")
    )
    return (
        jnp.stack(layer_rows),
        jnp.stack(input_rows),
        vector_part[0],
        vector_part[1],
        matrix_part[0],
        matrix_part[1],
        matrix_part[2],
        vector_part[2],
        vector_part[3],
        vector_part[4],
        matrix_part[3],
        matrix_part[4],
        matrix_part[5],
        vector_part[5],
    )


def solution(mesh):
    in_specs = (
        P("fsdp", ("ctx", "tp"), None),
        P("fsdp", ("ctx", "tp"), None),
        P("fsdp", None),
        P("fsdp", None),
        P("fsdp"),
        P("fsdp"),
        P("fsdp", None, "tp"),
        P(None, "tp", "fsdp"),
        P("tp", "fsdp"),
        P("fsdp"),
        P("fsdp"),
        P("fsdp"),
        P("fsdp", "tp"),
        P("tp", "fsdp"),
        P("tp", "fsdp"),
        P("fsdp"),
    )
    out_specs = (
        P("fsdp", ("ctx", "tp"), None),
        P("fsdp", ("ctx", "tp"), None),
        P("fsdp"),
        P("fsdp"),
        P("fsdp", None, "tp"),
        P(None, "tp", "fsdp"),
        P("tp", "fsdp"),
        P("fsdp"),
        P("fsdp"),
        P("fsdp"),
        P("fsdp", "tp"),
        P("tp", "fsdp"),
        P("tp", "fsdp"),
        P("fsdp"),
    )
    return jax.shard_map(shards, mesh=mesh, in_specs=in_specs, out_specs=out_specs, check_vma=False)
```

profile of v0, /device:TPU:0, one launch (start us, length us, event | category | flops | bytes accessed | tf_op | source)
XLA Modules:
  0.0 1361.0 jit_solution(4112993497679918625)
XLA Ops:
  10.5 12.6 all-gather.1
  23.2 8.0 all-gather
  38.3 12.4 all-gather.24.cloned.1.call-done
  50.6 23.0 %all-gather.22.cloned.1.call-done = bf16[1024,1024]{1,0:T(8,128)(2,1)} async-done(((bf16[256,1024]{1,0:T(8,128)(2,1)}), bf16[1024,1024]{1,0:T(8,128)(2,1)}) %all-gather.22.cloned.1.call-update) | async-done | bytes 2097168 | tf_op jit(solution)/shard_map/all_gather | solution.py:89
  80.3 13.2 all_gather.88
  106.8 16.4 %all_gather.91 = bf16[256,1024]{1,0:T(8,128)(2,1)} all-gather(bf16[256,256]{1,0:T(8,128)(2,1)S(1)} %copy-done.32), channel_id=1, replica_groups=mesh['fsdp'=4,'ctx'=2,'tp'=4] {'fsdp'}, dimensions={1}, use_global_device_ids=true | all-gather | bytes 655360 | tf_op jit(solution)/shard_map/all_gather | solution.py:61
  126.0 15.3 %fusion = (f32[4,1024]{1,0:T(4,128)S(1)}, f32[4,1024,2048]{2,1,0:T(8,128)}) fusion(pred[1024,2048]{1,0:T(8,128)(4,1)S(1)} %compare_and_fusion.1, bf16[1024,4,64]{0,2,1:T(8,128)(2,1)S(1)} %bitcast.222, bf16[2048,4,64]{0,2,1:T(8,128)(2,1)} %bitcast.224), kind=kOutput, calls=%fused_computation.10 | convolution fusion | flops 1098903552 | bytes 37240832 | tf_op jit(solution)/shard_map/qhd,khd->hqk/dot_general | solution.py:103
  141.3 15.2 %exponential_reduce_fusion.1 = f32[4,1024]{1,0:T(4,128)S(1)} fusion(f32[4,1024,2048]{2,1,0:T(8,128)} %get-tuple-element.98, f32[4,1024]{1,0:T(4,128)S(1)} %get-tuple-element.97, pred[1024,2048]{1,0:T(8,128)(4,1)S(1)} %compare_and_fusion.1), kind=kLoop, calls=%fused_computation.8 | loop fusion | flops 33550336 | bytes 35684352 | tf_op jit(solution)/shard_map/reduce_sum | solution.py:110
  156.5 16.0 %convolution_convert_fusion.15 = bf16[4,64,1024]{2,1,0:T(8,128)(2,1)} fusion(bf16[2048,4,64]{0,2,1:T(8,128)(2,1)} %bitcast.238, f32[4,1024,2048]{2,1,0:T(8,128)} %get-tuple-element.98, f32[4,1024]{1,0:T(4,128)S(1)} %log_add_fusion.1, pred[1024,2048]{1,0:T(8,128)(4,1)S(1)} %compare_and_fusion.1), kind=kOutput, calls=%fused_computation.90 | convolution fusion | flops 1107558400 | bytes 37240832 | tf_op jit(solution)/shard_map/hqk,khd->qhd/dot_general | solution.py:114
  180.4 15.7 %fusion.1 = (f32[4,1024]{1,0:T(4,128)S(1)}, f32[4,1024,2048]{2,1,0:T(8,128)}) fusion(pred[1024,2048]{1,0:T(8,128)(4,1)} %compare_and_fusion, bf16[1024,4,64]{0,2,1:T(8,128)(2,1)S(1)} %bitcast.220, bf16[2048,4,64]{0,2,1:T(8,128)(2,1)} %bitcast.226), kind=kOutput, calls=%fused_computation.11 | convolution fusion | flops 1098903552 | bytes 37240832 | tf_op jit(solution)/shard_map/qhd,khd->hqk/dot_general | solution.py:103
  196.1 15.8 %exponential_reduce_fusion = f32[4,1024]{1,0:T(4,128)S(1)} fusion(f32[4,1024,2048]{2,1,0:T(8,128)} %get-tuple-element.100, f32[4,1024]{1,0:T(4,128)S(1)} %get-tuple-element.99, pred[1024,2048]{1,0:T(8,128)(4,1)S(1)} %copy-done.1), kind=kLoop, calls=%fused_computation.5 | loop fusion | flops 33550336 | bytes 35684352 | tf_op jit(solution)/shard_map/reduce_sum | solution.py:110
  212.0 16.4 %convolution_convert_fusion.14 = bf16[4,64,1024]{2,1,0:T(8,128)(2,1)S(1)} fusion(bf16[2048,4,64]{0,2,1:T(8,128)(2,1)} %bitcast.240, f32[4,1024,2048]{2,1,0:T(8,128)} %get-tuple-element.100, f32[4,1024]{1,0:T(4,128)S(1)} %log_add_fusion, pred[1024,2048]{1,0:T(8,128)(4,1)} %compare_and_fusion), kind=kOutput, calls=%fused_computation.89 | convolution fusion | flops 1107558400 | bytes 37240832 | tf_op jit(solution)/shard_map/hqk,khd->qhd/dot_general | solution.py:114
  236.5 11.6 all-gather.4
  248.1 7.6 all-gather.3
  255.7 9.6 all-gather.2
  265.2 20.7 %reduce-scatter.37.cloned.1.call-done = f32[256,1024]{1,0:T(8,128)} async-done(((f32[1024,1024]{1,0:T(8,128)}), f32[256,1024]{1,0:T(8,128)}) %reduce-scatter.37.cloned.1.call-update) | async-done | bytes 1048592 | tf_op jit(solution)/shard_map/reduce_scatter | solution.py:123
  291.5 15.9 %all_gather.97 = bf16[16,64]{0,1:T(8,128)(2,1)S(1)} all-gather(bf16[16,16]{0,1:T(8,128)(2,1)S(1)} %copy.60), channel_id=1, replica_groups=mesh['fsdp'=4,'ctx'=2,'tp'=4] {'fsdp'}, dimensions={1}, use_global_device_ids=true | all-gather | bytes 2560 | tf_op jit(solution)/shard_map/all_gather | solution.py:66
  307.5 26.2 %all-gather.34.cloned.1.call-done = bf16[1024,1024]{1,0:T(8,128)(2,1)} async-done(((bf16[1024,256]{1,0:T(8,128)(2,1)}), bf16[1024,1024]{1,0:T(8,128)(2,1)}) %all-gather.34.cloned.1.call-update) | async-done | bytes 2097168 | tf_op jit(solution)/shard_map/all_gather | solution.py:67
  333.7 22.4 %all-gather.48.cloned.1.call-done = bf16[1024,1024]{1,0:T(8,128)(2,1)} async-done(((bf16[256,1024]{1,0:T(8,128)(2,1)}), bf16[1024,1024]{1,0:T(8,128)(2,1)}) %all-gather.48.cloned.1.call-update) | async-done | bytes 2097168 | tf_op jit(solution)/shard_map/all_gather | solution.py:145
  356.1 6.6 fusion.106
  362.7 40.5 %all-gather.32.cloned.1.call-done = bf16[1024,1024]{1,0:T(8,128)(2,1)} async-done(((bf16[256,1024]{1,0:T(8,128)(2,1)}), bf16[1024,1024]{1,0:T(8,128)(2,1)}) %all-gather.32.cloned.1.call-update) | async-done | bytes 2097168 | tf_op jit(solution)/shard_map/all_gather | solution.py:65
  403.2 23.5 %all-gather.42.cloned.1.call-done = bf16[1024,1024]{1,0:T(8,128)(2,1)} async-done(((bf16[256,1024]{1,0:T(8,128)(2,1)}), bf16[1024,1024]{1,0:T(8,128)(2,1)}) %all-gather.42.cloned.1.call-update) | async-done | bytes 2097168 | tf_op jit(solution)/shard_map/all_gather | solution.py:129
  426.7 6.6 fusion.105
  433.3 18.0 %all-gather.30.cloned.1.call-done = bf16[1024,1024]{1,0:T(8,128)(2,1)} async-done(((bf16[256,1024]{1,0:T(8,128)(2,1)}), bf16[1024,1024]{1,0:T(8,128)(2,1)}) %all-gather.30.cloned.1.call-update) | async-done | bytes 2097168 | tf_op jit(solution)/shard_map/all_gather | solution.py:129
  451.3 6.5 fusion.102
  457.8 17.5 %all-gather.44.cloned.1.call-done = bf16[1024,1024]{1,0:T(8,128)(2,1)} async-done(((bf16[256,1024]{1,0:T(8,128)(2,1)}), bf16[1024,1024]{1,0:T(8,128)(2,1)}) %all-gather.44.cloned.1.call-update) | async-done | bytes 2097168 | tf_op jit(solution)/shard_map/all_gather | solution.py:145
  475.3 15.5 %fusion.86 = (bf16[1024]{0:T(1024)(128)(2,1)}, bf16[1024,1024]{1,0:T(8,128)(2,1)}, bf16[1024]{0:T(1024)(128)(2,1)}, bf16[1024,1024]{1,0:T(8,128)(2,1)S(1)}) fusion(f32[1024,1024]{1,0:T(8,128)} %fusion.102, f32[1024]{0:T(1024)S(1)} %reshape.455, f32[1024,1024]{1,0:T(8,128)} %fusion.106, f32[1024,1024]{1,0:T(8,128)} %fusion.105, ...), kind=kOutput, calls=%fused_computation.206 | convolution fusion | flops 2202007552 | bytes 20979712 | tf_op jit(solution)/shard_map/td,fd->tf/dot_general | solution.py:148
  496.1 7.0 convolution_convert_fusion.8
  503.2 6.2 convolution_convert_fusion.7
  509.5 7.0 convolution_convert_fusion.9
  516.6 11.1 all-gather.5
  529.5 31.3 %reduce-scatter.39.cloned.1.call-done = bf16[256,1024]{1,0:T(8,128)(2,1)} async-done(((bf16[1024,1024]{1,0:T(8,128)(2,1)}), bf16[256,1024]{1,0:T(8,128)(2,1)}) %reduce-scatter.39.cloned.1.call-update) | async-done | bytes 524304 | tf_op jit(solution)/shard_map/reduce_scatter | solution.py:138
  560.8 33.6 %reduce-scatter.41.cloned.1.call-done = bf16[256,1024]{1,0:T(8,128)(2,1)} async-done(((bf16[1024,1024]{1,0:T(8,128)(2,1)}), bf16[256,1024]{1,0:T(8,128)(2,1)}) %reduce-scatter.41.cloned.1.call-update) | async-done | bytes 524304 | tf_op jit(solution)/shard_map/reduce_scatter | solution.py:154
  598.3 29.8 %reduce-scatter.35.cloned.1.call-done = bf16[256,1024]{1,0:T(8,128)(2,1)} async-done(((bf16[1024,1024]{1,0:T(8,128)(2,1)}), bf16[256,1024]{1,0:T(8,128)(2,1)}) %reduce-scatter.35.cloned.1.call-update) | async-done | bytes 524304 | tf_op jit(solution)/shard_map/reduce_scatter | solution.py:138
  639.3 20.3 %all-gather.50.cloned.1.call-done = bf16[1024,1024]{1,0:T(8,128)(2,1)} async-done(((bf16[256,1024]{1,0:T(8,128)(2,1)}), bf16[1024,1024]{1,0:T(8,128)(2,1)}) %all-gather.50.cloned.1.call-update) | async-done | bytes 2097168 | tf_op jit(solution)/shard_map/all_gather | solution.py:160
  661.9 16.0 %convolution_convert_fusion = bf16[4,64,2048]{2,1,0:T(8,128)(2,1)} fusion(bf16[1024,4,64]{0,2,1:T(8,128)(2,1)S(1)} %bitcast.244, f32[4,1024,2048]{2,1,0:T(8,128)} %get-tuple-element.100, f32[4,1024]{1,0:T(4,128)S(1)} %log_add_fusion, pred[1024,2048]{1,0:T(8,128)(4,1)} %compare_and_fusion), kind=kOutput, calls=%fused_computation.42 | convolution fusion | flops 1107820544 | bytes 37240832 | tf_op jit(solution)/shard_map/hqk,qhd->khd/dot_general | solution.py:168
  678.0 6.3 all-gather.46.cloned.1.call-done
  686.7 24.7 %multiply_reduce_fusion.1 = (f32[4,1024]{1,0:T(4,128)S(1)}, f32[4,1024,2048]{2,1,0:T(8,128)}) fusion(f32[4,1024,2048]{2,1,0:T(8,128)} %get-tuple-element.98, f32[4,1024]{1,0:T(4,128)S(1)} %log_add_fusion.1, pred[1024,2048]{1,0:T(8,128)(4,1)S(1)} %compare_and_fusion.1, bf16[1024,4,64]{0,2,1:T(8,128)(2,1)S(1)} %bitcast.246, bf16[2048,4,64]{0,2,1:T(8,128)(2,1)S(1)} %bitcast.239), kind=kOutput, calls=%fused_computation.3 | convolution fusion | flops 1115680768 | bytes 70811648 | tf_op jit(solution)/shard_map/qhd,khd->hqk/dot_general | solution.py:171
  711.4 15.2 %convolution_convert_fusion.1 = bf16[4,64,2048]{2,1,0:T(8,128)(2,1)} fusion(bf16[1024,4,64]{0,2,1:T(8,128)(2,1)S(1)} %bitcast.247, f32[4,1024,2048]{2,1,0:T(8,128)} %get-tuple-element.98, f32[4,1024]{1,0:T(4,128)S(1)} %log_add_fusion.1, pred[1024,2048]{1,0:T(8,128)(4,1)S(1)} %compare_and_fusion.1), kind=kOutput, calls=%fused_computation.43 | convolution fusion | flops 1107820544 | bytes 37240832 | tf_op jit(solution)/shard_map/hqk,qhd->khd/dot_general | solution.py:168
  727.1 27.8 %multiply_convert_fusion.1 = bf16[4,1024,2048]{2,1,0:T(8,128)(2,1)} fusion(f32[4,1024,2048]{2,1,0:T(8,128)} %get-tuple-element.102, f32[4,1024,2048]{2,1,0:T(8,128)} %get-tuple-element.98, f32[4,1024]{1,0:T(4,128)S(1)} %get-tuple-element.101, f32[4,1024]{1,0:T(4,128)S(1)} %log_add_fusion.1, pred[1024,2048]{1,0:T(8,128)(4,1)S(1)} %compare_and_fusion.1), kind=kLoop, calls=%fused_computation.2 | loop fusion | flops 50331648 | bytes 86016000 | tf_op jit(solution)/shard_map/convert_element_type | solution.py:175
  754.9 27.0 %multiply_reduce_fusion = (f32[4,1024]{1,0:T(4,128)S(1)}, f32[4,1024,2048]{2,1,0:T(8,128)}) fusion(f32[4,1024,2048]{2,1,0:T(8,128)} %get-tuple-element.100, f32[4,1024]{1,0:T(4,128)S(1)} %log_add_fusion, pred[1024,2048]{1,0:T(8,128)(4,1)} %compare_and_fusion, bf16[1024,4,64]{0,2,1:T(8,128)(2,1)} %bitcast.245, bf16[2048,4,64]{0,2,1:T(8,128)(2,1)} %bitcast.241), kind=kOutput, calls=%fused_computation.1 | convolution fusion | flops 1115680768 | bytes 70811648 | tf_op jit(solution)/shard_map/qhd,khd->hqk/dot_general | solution.py:171
  785.9 28.9 %multiply_convert_fusion = bf16[4,1024,2048]{2,1,0:T(8,128)(2,1)} fusion(f32[4,1024,2048]{2,1,0:T(8,128)} %get-tuple-element.104, f32[4,1024,2048]{2,1,0:T(8,128)} %get-tuple-element.100, f32[4,1024]{1,0:T(4,128)S(1)} %get-tuple-element.103, f32[4,1024]{1,0:T(4,128)S(1)} %log_add_fusion, pred[1024,2048]{1,0:T(8,128)(4,1)} %compare_and_fusion), kind=kLoop, calls=%fused_computation | loop fusion | flops 50331648 | bytes 86016000 | tf_op jit(solution)/shard_map/convert_element_type | solution.py:175
  814.8 9.9 fusion.17
  826.7 6.6 convolution_convert_fusion.2
  833.4 7.4 convolution_convert_fusion.3
  840.9 5.4 convolution_convert_fusion.4
  846.4 5.9 convolution_convert_fusion.5
  859.1 11.2 bitcast_reduce_fusion.1
  870.3 11.1 bitcast_reduce_fusion
  910.9 20.6 %reduce-scatter.71.cloned.1.call-done = bf16[1024,256]{1,0:T(8,128)(2,1)} async-done(((bf16[1024,1024]{1,0:T(8,128)(2,1)}), bf16[1024,256]{1,0:T(8,128)(2,1)}) %reduce-scatter.71.cloned.1.call-update) | async-done | bytes 524304 | tf_op jit(solution)/shard_map/reduce_scatter | solution.py:264
  931.4 45.2 %reduce-scatter.69.cloned.1.call-done = bf16[1024,256]{1,0:T(8,128)(2,1)} async-done(((bf16[1024,1024]{1,0:T(8,128)(2,1)}), bf16[1024,256]{1,0:T(8,128)(2,1)}) %reduce-scatter.69.cloned.1.call-update) | async-done | bytes 524304 | tf_op jit(solution)/shard_map/reduce_scatter | solution.py:264
  978.7 42.9 %reduce-scatter.67.cloned.1.call-done = bf16[256,1024]{1,0:T(8,128)(2,1)} async-done(((bf16[1024,1024]{1,0:T(8,128)(2,1)}), bf16[256,1024]{1,0:T(8,128)(2,1)}) %reduce-scatter.67.cloned.1.call-update) | async-done | bytes 524304 | tf_op jit(solution)/shard_map/reduce_scatter | solution.py:258
  1021.6 45.2 %reduce-scatter.65.cloned.1.call-done = bf16[256,1024]{1,0:T(8,128)(2,1)} async-done(((bf16[1024,1024]{1,0:T(8,128)(2,1)}), bf16[256,1024]{1,0:T(8,128)(2,1)}) %reduce-scatter.65.cloned.1.call-update) | async-done | bytes 524304 | tf_op jit(solution)/shard_map/reduce_scatter | solution.py:258
  1069.0 21.1 %reduce-scatter.61.cloned.1.call-done = bf16[256,256]{1,0:T(8,128)(2,1)} async-done(((bf16[256,1024]{1,0:T(8,128)(2,1)}), bf16[256,256]{1,0:T(8,128)(2,1)}) %reduce-scatter.61.cloned.1.call-update) | async-done | bytes 131088 | tf_op jit(solution)/shard_map/reduce_scatter | solution.py:246
  1090.1 22.3 %reduce-scatter.63.cloned.1.call-done = bf16[256,256]{1,0:T(8,128)(2,1)} async-done(((bf16[256,1024]{1,0:T(8,128)(2,1)}), bf16[256,256]{1,0:T(8,128)(2,1)}) %reduce-scatter.63.cloned.1.call-update) | async-done | bytes 131088 | tf_op jit(solution)/shard_map/reduce_scatter | solution.py:246
  1114.0 18.0 %reduce-scatter.73.cloned.1.call-done = bf16[16,8]{1,0:T(8,128)(2,1)} async-done(((bf16[64,8]{1,0:T(8,128)(2,1)}), bf16[16,8]{1,0:T(8,128)(2,1)}) %reduce-scatter.73.cloned.1.call-update) | async-done | bytes 272
  1132.9 18.7 %reduce-scatter.75.cloned.1.call-done = bf16[16,8]{1,0:T(8,128)(2,1)} async-done(((bf16[64,8]{1,0:T(8,128)(2,1)}), bf16[16,8]{1,0:T(8,128)(2,1)}) %reduce-scatter.75.cloned.1.call-update) | async-done | bytes 272
  1158.7 28.7 %reduce-scatter.57.cloned.1.call-done = bf16[256,3,256]{2,0,1:T(8,128)(2,1)} async-done(((bf16[1024,3,256]{2,0,1:T(8,128)(2,1)}), bf16[256,3,256]{2,0,1:T(8,128)(2,1)}) %reduce-scatter.57.cloned.1.call-update) | async-done | bytes 393232 | tf_op jit(solution)/shard_map/reduce_scatter | solution.py:240
  1187.5 36.5 %reduce-scatter.59.cloned.1.call-done = bf16[256,3,256]{2,0,1:T(8,128)(2,1)} async-done(((bf16[1024,3,256]{2,0,1:T(8,128)(2,1)}), bf16[256,3,256]{2,0,1:T(8,128)(2,1)}) %reduce-scatter.59.cloned.1.call-update) | async-done | bytes 393232 | tf_op jit(solution)/shard_map/reduce_scatter | solution.py:240
  1225.9 31.2 %reduce-scatter.47.cloned.1.call-done = bf16[256,1024]{1,0:T(8,128)(2,1)} async-done(((bf16[1024,1024]{1,0:T(8,128)(2,1)}), bf16[256,1024]{1,0:T(8,128)(2,1)}) %reduce-scatter.47.cloned.1.call-update) | async-done | bytes 524304 | tf_op jit(solution)/shard_map/reduce_scatter | solution.py:208
  1257.1 33.6 %reduce-scatter.55.cloned.1.call-done = bf16[256,1024]{1,0:T(8,128)(2,1)} async-done(((bf16[1024,1024]{1,0:T(8,128)(2,1)}), bf16[256,1024]{1,0:T(8,128)(2,1)}) %reduce-scatter.55.cloned.1.call-update) | async-done | bytes 524304 | tf_op jit(solution)/shard_map/reduce_scatter | solution.py:208
  1297.2 19.0 %all-reduce.13 = (bf16[1024]{0:T(1024)(128)(2,1)S(1)}, bf16[1024]{0:T(1024)(128)(2,1)S(1)}, bf16[1024]{0:T(1024)(128)(2,1)S(1)}, bf16[1024]{0:T(1024)(128)(2,1)S...) all-reduce(bf16[1024]{0:T(1024)(128)(2,1)S(1)} %get-tuple-element.2, ...), channel_id=15, replica_groups=mesh['fsdp'=4,'ctx'=2,'tp'=4] {'fsdp'}, use_global_device_ids=true, to_apply=%region_41.42.clone | all-reduce | flops 12288 | bytes 49152
  1316.7 12.7 all-reduce.12
  1332.9 13.1 all-reduce.18.cloned.1.call-done
  (368 shorter events, 157.5 us)
Async XLA Ops:
  7.2 43.5 %all-gather.24.cloned.1.call-start = ((), (), s32[]{:S(2)}) async-start(), calls=%async_computation.25 | async-start | bytes 1966080 | tf_op jit(solution)/shard_map/all_gather | solution.py:59
  9.2 64.4 %all-gather.22.cloned.1.call-start = ((), (), s32[]{:S(2)}) async-start(), calls=%async_computation.24 | async-start | bytes 2621440 | tf_op jit(solution)/shard_map/all_gather | solution.py:89
  37.5 60.9 %all-gather.36.cloned.1.call-start = ((), (), s32[]{:S(2)}) async-start(), calls=%async_computation.33 | async-start | bytes 2621440 | tf_op jit(solution)/shard_map/all_gather | solution.py:89
  38.2 87.8 %all-gather.28.cloned.1.call-start = ((), (), s32[]{:S(2)}) async-start(), calls=%async_computation.27 | async-start | bytes 1572864 | tf_op jit(solution)/shard_map/all_gather | solution.py:95
  80.1 76.4 %all-gather.26.cloned.1.call-start = ((), (), s32[]{:S(2)}) async-start(), calls=%async_computation.26 | async-start | bytes 1572864 | tf_op jit(solution)/shard_map/all_gather | solution.py:96
  103.9 37.4 %copy-start.9 = (bf16[1024,256]{0,1:T(8,128)(2,1)}, bf16[1024,256]{0,1:T(8,128)(2,1)S(1)}, u32[]{:S(2)}) copy-start(bf16[1024,256]{0,1:T(8,128)(2,1)S(1)} %get-tuple-element.94) | copy-start | bytes 1572868
  103.9 76.5 %copy-start.7 = (bf16[1024,256]{0,1:T(8,128)(2,1)}, bf16[1024,256]{0,1:T(8,128)(2,1)S(1)}, u32[]{:S(2)}) copy-start(bf16[1024,256]{0,1:T(8,128)(2,1)S(1)} %get-tuple-element.71) | copy-start | bytes 1572868
  103.9 76.4 %all-gather.40.cloned.1.call-start = ((), (), s32[]{:S(2)}) async-start(), calls=%async_computation.35 | async-start | bytes 1572864 | tf_op jit(solution)/shard_map/all_gather | solution.py:95
  106.4 105.6 %all-gather.38.cloned.1.call-start = ((), (), s32[]{:S(2)}) async-start(), calls=%async_computation.34 | async-start | bytes 1572864 | tf_op jit(solution)/shard_map/all_gather | solution.py:96
  125.8 139.5 %reduce-scatter.33.cloned.1.call-start = ((), (), s32[]{:S(2)}) async-start(), calls=%async_computation.28 | async-start | bytes 5242880 | tf_op jit(solution)/shard_map/reduce_scatter | solution.py:123
  176.3 109.6 %reduce-scatter.37.cloned.1.call-start = ((), (), s32[]{:S(2)}) async-start(), calls=%async_computation.36 | async-start | bytes 5242880 | tf_op jit(solution)/shard_map/reduce_scatter | solution.py:123
  231.9 54.0 %copy-start.2 = (bf16[2,256,1024]{2,1,0:T(8,128)(2,1)S(1)}, bf16[2,256,1024]{2,1,0:T(8,128)(2,1)}, u32[]{:S(2)}) copy-start(bf16[2,256,1024]{2,1,0:T(8,128)(2,1)} %param.16) | copy-start | bytes 3145732
  232.0 101.8 %all-gather.34.cloned.1.call-start = ((), (), s32[]{:S(2)}) async-start(), calls=%async_computation.31 | async-start | bytes 2621440 | tf_op jit(solution)/shard_map/all_gather | solution.py:67
  232.6 123.5 %all-gather.48.cloned.1.call-start = ((), (), s32[]{:S(2)}) async-start(), calls=%async_computation.45 | async-start | bytes 2621440 | tf_op jit(solution)/shard_map/all_gather | solution.py:145
  235.8 167.4 %all-gather.32.cloned.1.call-start = ((), (), s32[]{:S(2)}) async-start(), calls=%async_computation.30 | async-start | bytes 2621440 | tf_op jit(solution)/shard_map/all_gather | solution.py:65
  236.4 190.3 %all-gather.42.cloned.1.call-start = ((), (), s32[]{:S(2)}) async-start(), calls=%async_computation.37 | async-start | bytes 2621440 | tf_op jit(solution)/shard_map/all_gather | solution.py:129
  290.2 161.1 %all-gather.30.cloned.1.call-start = ((), (), s32[]{:S(2)}) async-start(), calls=%async_computation.29 | async-start | bytes 2621440 | tf_op jit(solution)/shard_map/all_gather | solution.py:129
  290.8 184.6 %all-gather.44.cloned.1.call-start = ((), (), s32[]{:S(2)}) async-start(), calls=%async_computation.39 | async-start | bytes 2621440 | tf_op jit(solution)/shard_map/all_gather | solution.py:145
  291.3 236.4 %reduce-scatter.49.cloned.1.call-start = ((), (), s32[]{:S(2)}) async-start(), calls=%async_computation.46 | async-start | bytes 2621440 | tf_op jit(solution)/shard_map/reduce_scatter | solution.py:154
  307.5 202.0 %copy-start.55 = (f32[1024]{0:T(1024)}, f32[1024]{0:T(1024)S(1)}, u32[]{:S(2)}) copy-start(f32[1024]{0:T(1024)S(1)} %reshape.455) | copy-start | bytes 12292
  495.9 64.9 %reduce-scatter.39.cloned.1.call-start = ((), (), s32[]{:S(2)}) async-start(), calls=%async_computation.38 | async-start | bytes 2621440 | tf_op jit(solution)/shard_map/reduce_scatter | solution.py:138
  503.2 91.2 %reduce-scatter.41.cloned.1.call-start = ((), (), s32[]{:S(2)}) async-start(), calls=%async_computation.40 | async-start | bytes 2621440 | tf_op jit(solution)/shard_map/reduce_scatter | solution.py:154
  509.5 118.6 %reduce-scatter.35.cloned.1.call-start = ((), (), s32[]{:S(2)}) async-start(), calls=%async_computation.32 | async-start | bytes 2621440 | tf_op jit(solution)/shard_map/reduce_scatter | solution.py:138
  516.5 77.8 %copy-start.5 = (f32[256,1024]{1,0:T(8,128)S(1)}, f32[256,1024]{1,0:T(8,128)}, u32[]{:S(2)}) copy-start(f32[256,1024]{1,0:T(8,128)} %copy-done.4) | copy-start | bytes 3145732
  516.6 143.0 %all-gather.50.cloned.1.call-start = ((), (), s32[]{:S(2)}) async-start(), calls=%async_computation.47 | async-start | bytes 2621440 | tf_op jit(solution)/shard_map/all_gather | solution.py:160
  636.8 47.4 %all-gather.46.cloned.1.call-start = ((), (), s32[]{:S(2)}) async-start(), calls=%async_computation.41 | async-start | bytes 2621440 | tf_op jit(solution)/shard_map/all_gather | solution.py:160
  639.0 242.4 %reduce-scatter.53.cloned.1.call-start = ((), (), s32[]{:S(2)}) async-start(), calls=%async_computation.49 | async-start | bytes 1572864 | tf_op jit(solution)/shard_map/reduce_scatter | solution.py:189
  677.9 204.8 %reduce-scatter.45.cloned.1.call-start = ((), (), s32[]{:S(2)}) async-start(), calls=%async_computation.43 | async-start | bytes 1572864 | tf_op jit(solution)/shard_map/reduce_scatter | solution.py:189
  726.6 159.2 %reduce-scatter.43.cloned.1.call-start = ((), (), s32[]{:S(2)}) async-start(), calls=%async_computation.42 | async-start | bytes 1572864 | tf_op jit(solution)/shard_map/reduce_scatter | solution.py:183
  754.9 27.0 %copy-start = (bf16[4,1024,2048]{2,1,0:T(8,128)(2,1)S(1)}, bf16[4,1024,2048]{2,1,0:T(8,128)(2,1)}, u32[]{:S(2)}) copy-start(bf16[4,1024,2048]{2,1,0:T(8,128)(2,1)} %multiply_convert_fusion.1) | copy-start | bytes 50331652
  754.9 27.0 %copy-start.10 = (bf16[1024,256]{0,1:T(8,128)(2,1)S(1)}, bf16[1024,256]{0,1:T(8,128)(2,1)}, u32[]{:S(2)}) copy-start(bf16[1024,256]{0,1:T(8,128)(2,1)} %copy-done.9) | copy-start | bytes 1572868
  785.9 105.4 %reduce-scatter.51.cloned.1.call-start = ((), (), s32[]{:S(2)}) async-start(), calls=%async_computation.48 | async-start | bytes 1572864 | tf_op jit(solution)/shard_map/reduce_scatter | solution.py:183
  785.9 28.9 %copy-start.8 = (bf16[1024,256]{0,1:T(8,128)(2,1)S(1)}, bf16[1024,256]{0,1:T(8,128)(2,1)}, u32[]{:S(2)}) copy-start(bf16[1024,256]{0,1:T(8,128)(2,1)} %copy-done.7) | copy-start | bytes 1572868
  824.8 83.2 %reduce-scatter.79.cloned.1.call-start = ((), (), s32[]{:S(2)}) async-start(), calls=%async_computation.62 | async-start | bytes 20480
  825.6 83.1 %reduce-scatter.77.cloned.1.call-start = ((), (), s32[]{:S(2)}) async-start(), calls=%async_computation.61 | async-start | bytes 20480
  826.5 104.9 %reduce-scatter.71.cloned.1.call-start = ((), (), s32[]{:S(2)}) async-start(), calls=%async_computation.58 | async-start | bytes 2621440 | tf_op jit(solution)/shard_map/reduce_scatter | solution.py:264
  833.4 143.2 %reduce-scatter.69.cloned.1.call-start = ((), (), s32[]{:S(2)}) async-start(), calls=%async_computation.57 | async-start | bytes 2621440 | tf_op jit(solution)/shard_map/reduce_scatter | solution.py:264
  840.8 180.8 %reduce-scatter.67.cloned.1.call-start = ((), (), s32[]{:S(2)}) async-start(), calls=%async_computation.56 | async-start | bytes 2621440 | tf_op jit(solution)/shard_map/reduce_scatter | solution.py:258
  846.3 220.4 %reduce-scatter.65.cloned.1.call-start = ((), (), s32[]{:S(2)}) async-start(), calls=%async_computation.55 | async-start | bytes 2621440 | tf_op jit(solution)/shard_map/reduce_scatter | solution.py:258
  852.4 237.7 %reduce-scatter.61.cloned.1.call-start = ((), (), s32[]{:S(2)}) async-start(), calls=%async_computation.53 | async-start | bytes 655360 | tf_op jit(solution)/shard_map/reduce_scatter | solution.py:246
  855.7 256.7 %reduce-scatter.63.cloned.1.call-start = ((), (), s32[]{:S(2)}) async-start(), calls=%async_computation.54 | async-start | bytes 655360 | tf_op jit(solution)/shard_map/reduce_scatter | solution.py:246
  870.3 261.8 %reduce-scatter.73.cloned.1.call-start = ((), (), s32[]{:S(2)}) async-start(), calls=%async_computation.59 | async-start | bytes 20480
  884.8 266.8 %reduce-scatter.75.cloned.1.call-start = ((), (), s32[]{:S(2)}) async-start(), calls=%async_computation.60 | async-start | bytes 20480
  885.7 301.7 %reduce-scatter.57.cloned.1.call-start = ((), (), s32[]{:S(2)}) async-start(), calls=%async_computation.51 | async-start | bytes 1966080 | tf_op jit(solution)/shard_map/reduce_scatter | solution.py:240
  891.2 332.7 %reduce-scatter.59.cloned.1.call-start = ((), (), s32[]{:S(2)}) async-start(), calls=%async_computation.52 | async-start | bytes 1966080 | tf_op jit(solution)/shard_map/reduce_scatter | solution.py:240
  896.4 360.7 %reduce-scatter.47.cloned.1.call-start = ((), (), s32[]{:S(2)}) async-start(), calls=%async_computation.44 | async-start | bytes 2621440 | tf_op jit(solution)/shard_map/reduce_scatter | solution.py:208
  901.6 389.1 %reduce-scatter.55.cloned.1.call-start = ((), (), s32[]{:S(2)}) async-start(), calls=%async_computation.50 | async-start | bytes 2621440 | tf_op jit(solution)/shard_map/reduce_scatter | solution.py:208
  906.7 439.3 %all-reduce.18.cloned.1.call-start = ((), (), s32[]{:S(2)}) async-start(), calls=%async_computation.63 | async-start | bytes 3145728 | tf_op jit(solution)/shard_map/psum | solution.py:273
  909.8 380.9 %copy-start.3 = (bf16[2,256,1024]{2,1,0:T(8,128)(2,1)S(1)}, bf16[2,256,1024]{2,1,0:T(8,128)(2,1)}, u32[]{:S(2)}) copy-start(bf16[2,256,1024]{2,1,0:T(8,128)(2,1)} %param.16) | copy-start | bytes 3145732
  909.8 380.9 %copy-start.34 = (f32[4,1,256]{2,1,0:T(1,128)S(1)}, f32[4,1,256]{2,1,0:T(1,128)}, u32[]{:S(2)}) copy-start(f32[4,1,256]{2,1,0:T(1,128)} %copy-done.33) | copy-start | bytes 12292
  909.8 380.9 %copy-start.36 = (f32[256]{0:T(256)S(1)}, f32[256]{0:T(256)}, u32[]{:S(2)}) copy-start(f32[256]{0:T(256)} %copy-done.35) | copy-start | bytes 3076
  909.8 380.9 %copy-start.38 = (f32[256]{0:T(256)S(1)}, f32[256]{0:T(256)}, u32[]{:S(2)}) copy-start(f32[256]{0:T(256)} %copy-done.37) | copy-start | bytes 3076
  910.9 381.5 %copy-start.47 = (f32[256]{0:T(256)S(1)}, f32[256]{0:T(256)}, u32[]{:S(2)}) copy-start(f32[256]{0:T(256)} %copy-done.46) | copy-start | bytes 3076
  910.9 381.6 %copy-start.45 = (f32[256]{0:T(256)S(1)}, f32[256]{0:T(256)}, u32[]{:S(2)}) copy-start(f32[256]{0:T(256)} %copy-done.44) | copy-start | bytes 3076
  978.7 316.0 %copy-start.41 = (f32[256]{0:T(256)S(1)}, f32[256]{0:T(256)}, u32[]{:S(2)}) copy-start(f32[256]{0:T(256)} %copy-done.40) | copy-start | bytes 3076
  978.7 316.0 %copy-start.43 = (f32[256]{0:T(256)S(1)}, f32[256]{0:T(256)}, u32[]{:S(2)}) copy-start(f32[256]{0:T(256)} %copy-done.42) | copy-start | bytes 3076
  1068.9 228.2 %copy-start.48 = (bf16[1024]{0:T(1024)(128)(2,1)S(1)}, bf16[1024]{0:T(1024)(128)(2,1)}, u32[]{:S(2)}) copy-start(bf16[1024]{0:T(1024)(128)(2,1)} %get-tuple-element.26) | copy-start | bytes 6148
  1068.9 228.2 %copy-start.49 = (bf16[1024]{0:T(1024)(128)(2,1)S(1)}, bf16[1024]{0:T(1024)(128)(2,1)}, u32[]{:S(2)}) copy-start(bf16[1024]{0:T(1024)(128)(2,1)} %get-tuple-element.27) | copy-start | bytes 6148
  1068.9 228.2 %copy-start.50 = (bf16[1024]{0:T(1024)(128)(2,1)S(1)}, bf16[1024]{0:T(1024)(128)(2,1)}, u32[]{:S(2)}) copy-start(bf16[1024]{0:T(1024)(128)(2,1)} %get-tuple-element.16) | copy-start | bytes 6148
  1068.9 228.2 %copy-start.51 = (bf16[1024]{0:T(1024)(128)(2,1)S(1)}, bf16[1024]{0:T(1024)(128)(2,1)}, u32[]{:S(2)}) copy-start(bf16[1024]{0:T(1024)(128)(2,1)} %get-tuple-element.61) | copy-start | bytes 6148
  1068.9 228.2 %copy-start.52 = (bf16[1024]{0:T(1024)(128)(2,1)S(1)}, bf16[1024]{0:T(1024)(128)(2,1)}, u32[]{:S(2)}) copy-start(bf16[1024]{0:T(1024)(128)(2,1)} %get-tuple-element.77) | copy-start | bytes 6148
  1069.0 228.2 %copy-start.53 = (bf16[1024]{0:T(1024)(128)(2,1)S(1)}, bf16[1024]{0:T(1024)(128)(2,1)}, u32[]{:S(2)}) copy-start(bf16[1024]{0:T(1024)(128)(2,1)} %get-tuple-element.14) | copy-start | bytes 6148
  1114.0 215.4 %copy-start.11 = (f32[256,1024]{1,0:T(8,128)S(1)}, f32[256,1024]{1,0:T(8,128)}, u32[]{:S(2)}) copy-start(f32[256,1024]{1,0:T(8,128)} %get-tuple-element.62) | copy-start | bytes 3145732
  1114.0 215.4 %copy-start.13 = (f32[256,1024]{1,0:T(8,128)S(1)}, f32[256,1024]{1,0:T(8,128)}, u32[]{:S(2)}) copy-start(f32[256,1024]{1,0:T(8,128)} %copy-done.12) | copy-start | bytes 3145732
  (47 other events, 313.9 us)
Sparse Core Ops, SparseCore 0:
  10.1 40.4 all-gather.23
  52.8 20.7 all-gather.21
  75.7 22.5 all-gather.35
  100.3 21.2 all-gather.27
  123.6 21.2 all-gather.25
  146.9 21.2 all-gather.39
  170.3 21.2 all-gather.37
  194.1 44.5 reduce-scatter.32
  241.3 44.5 reduce-scatter.36
  287.3 46.3 all-gather.33
  335.3 20.7 all-gather.47
  357.5 45.6 all-gather.31
  405.3 21.3 all-gather.41
  428.7 22.5 all-gather.29
  452.7 22.5 all-gather.43
  496.0 31.1 reduce-scatter.48
  529.6 31.1 reduce-scatter.38
  563.2 31.1 reduce-scatter.40
  596.9 31.1 reduce-scatter.34
  637.0 22.5 all-gather.49
  661.7 22.5 all-gather.45
  686.5 20.3 reduce-scatter.52
  726.7 20.3 reduce-scatter.44
  786.0 20.7 reduce-scatter.42
  824.9 20.9 reduce-scatter.50
  848.5 19.2 reduce-scatter.78
  869.9 17.3 reduce-scatter.76
  889.6 41.8 reduce-scatter.70
  933.7 42.8 reduce-scatter.68
  978.7 42.8 reduce-scatter.66
  1023.9 42.8 reduce-scatter.64
  1069.0 21.0 reduce-scatter.60
  1092.2 20.1 reduce-scatter.62
  1114.6 17.3 reduce-scatter.72
  1134.3 17.3 reduce-scatter.74
  1153.8 33.5 reduce-scatter.56
  1189.6 34.2 reduce-scatter.58
  1227.0 30.0 reduce-scatter.46
  1259.5 31.1 reduce-scatter.54
  1294.3 51.6 all-reduce.17
where the time goes:
time: 1370 us; the launch traced here: 1360 us
  waiting for transfers between devices  710 us (52%)
  matrix products  309 us (23%)
  other arithmetic  155 us (11%)
  blocking collectives  143 us (10%)
  local copies, waits for them, and re-layouts  24.3 us (2%)
  between operations  16.8 us (1%)
    reduce_scatter x2, waiting for transfers between devices, shards(): lax.psum_scatter(grad_set[8].astype(jnp.bfloat16), 'fsdp', scatter_dimens...  88 us
    reduce_scatter x2, waiting for transfers between devices, shards(): lax.psum_scatter(grad_set[10].astype(jnp.bfloat16), 'fsdp', scatter_dimen...  65.7 us
    reduce_scatter x2, waiting for transfers between devices, shards(): lax.psum_scatter(grad_set[2].astype(jnp.bfloat16), 'fsdp', scatter_dimens...  65.2 us
    reduce_scatter x2, waiting for transfers between devices, shards(): lax.psum_scatter(first_part.astype(jnp.bfloat16), 'tp', scatter_dimension...  64.7 us
    reduce_scatter x2, waiting for transfers between devices, shards(): lax.psum_scatter(feed_part.astype(jnp.bfloat16), 'tp', scatter_dimension=...  61.1 us
    convert_element_type x2, other arithmetic, shards(): score_grad = (attention * (attention_grad - row_delta)).astype(bf16)  56.7 us
    dot_general x2, matrix products, shards(): jnp.einsum('qhd,khd->hqk', mixed_grad, value_heads, preferred_element_typ...  51.6 us
    reduce_scatter x2, waiting for transfers between devices, shards(): lax.psum_scatter(grad_set[4].astype(jnp.bfloat16), 'fsdp', scatter_dimens...  43.4 us
  transfers between devices with their start and end apart: 40, of which 28 were waited for; matrix products, arithmetic and copies ran while one was open for 33% of the time, Pallas kernels for 0%

commit v1 on v0

v1 whole, which is shorter than its diff:
```python
import functools

import jax
import jax.numpy as jnp
from jax import lax
from jax.experimental import pallas as pl
from jax.experimental.pallas import tpu as pltpu
from jax.sharding import PartitionSpec as P

EPSILON = 1e-05
NEGATIVE = -1e30
GELU_SCALE = 0.7978845608028654
GELU_CUBIC = 0.044715
DEAL = 64
f32 = jnp.float32
bf16 = jnp.bfloat16
VM = pl.BlockSpec(memory_space=pltpu.VMEM)
SM = pl.BlockSpec(memory_space=pltpu.SMEM)


def dot(a, b):
    return jnp.dot(a, b, preferred_element_type=f32)


def dot_t(a, b):
    return lax.dot_general(a, b, (((1,), (1,)), ((), ())), preferred_element_type=f32)


def t_dot(a, b):
    return lax.dot_general(a, b, (((0,), (0,)), ((), ())), preferred_element_type=f32)


def tile_bounds(info_ref, tile, q_tile, key_tile, blocks):
    per = q_tile // DEAL
    base = 2 * blocks
    lane = lax.broadcasted_iota(jnp.int32, (1, q_tile), 1)
    end_one, end_two = info_ref[4 * blocks], info_ref[4 * blocks + 1]
    start = jnp.zeros((1, q_tile), jnp.int32)
    for b in range(per):
        start = jnp.where(
            lane // DEAL == b, (info_ref[base + tile * per + b] - b) * DEAL, start
        )
    position = start + lane
    low = jnp.where(position >= end_two, end_two, jnp.where(position >= end_one, end_one, 0))
    first = info_ref[base + tile * per] * DEAL
    last = info_ref[base + tile * per + per - 1] * DEAL + DEAL - 1
    first_low = jnp.where(first >= end_two, end_two, jnp.where(first >= end_one, end_one, 0))
    return position, low, first_low // key_tile, last // key_tile + 1


def block_rows(refs, i):
    per = refs[0].shape[0] // DEAL
    return refs[i // per], slice((i % per) * DEAL, (i % per + 1) * DEAL)


def rows_at(block):
    return pl.ds(pl.multiple_of(block * DEAL, DEAL), DEAL)


def block_diag(src, out_ref, heads, size, q_tile):
    row = lax.broadcasted_iota(jnp.int32, (heads * size, q_tile), 0) // size
    for h in range(heads):
        out_ref[:, h * q_tile : (h + 1) * q_tile] = jnp.where(row == h, src, jnp.zeros_like(src))


def load_sorted(info_ref, kv_refs, width, blocks, ks, vs):
    for i in range(2 * blocks):
        ref, rows = block_rows(kv_refs, i)
        to = rows_at(info_ref[i])
        ks[to, :] = ref[rows, :width]
        vs[to, :] = ref[rows, width:]


def fwd_kernel(parts, heads, size, q_tile, key_tile, *refs):
    info_ref = refs[0]
    q_refs = refs[1 : 1 + parts]
    kv_refs = refs[1 + parts : 1 + 3 * parts]
    out_refs = refs[1 + 3 * parts : 1 + 4 * parts]
    ot_ref, log_ref, ks, vt, vs, qs, qtd, os = refs[1 + 4 * parts :]
    width = heads * size
    qn = qs.shape[0]
    blocks = qn // DEAL
    load_sorted(info_ref, kv_refs, width, blocks, ks, vs)
    for i in range(blocks):
        ref, rows = block_rows(q_refs, i)
        qs[rows_at(info_ref[3 * blocks + i]), :] = ref[rows, :] * bf16(size**-0.5)
    kn = ks.shape[0]
    for t in range(kn // key_tile):
        vt[t] = vs[t * key_tile : (t + 1) * key_tile, :].T
    for t in range(qn // q_tile):
        position, low, k_lo, k_hi = tile_bounds(info_ref, t, q_tile, key_tile, blocks)
        block_diag(qs[t * q_tile : (t + 1) * q_tile, :].T, qtd, heads, size, q_tile)
        sub = lax.broadcasted_iota(jnp.int32, (key_tile, q_tile), 0)

        def body(k, carry):
            rows = pl.ds(pl.multiple_of(k * key_tile, key_tile), key_tile)
            kt = ks[rows, :]
            vtt = vt[k]
            kp = sub + k * key_tile
            ok = (kp <= position) & (kp >= low)
            new = []
            for h in range(heads):
                m, total, acc = carry[h]
                s = dot(kt, qtd[:, h * q_tile : (h + 1) * q_tile])
                s = jnp.where(ok, s, NEGATIVE)
                m_new = jnp.maximum(m, jnp.max(s, axis=0, keepdims=True))
                alpha = jnp.exp(m - m_new)
                p = jnp.exp(s - m_new)
                total = total * alpha + jnp.sum(p, axis=0, keepdims=True)
                acc = acc * alpha + dot(vtt[h * size : (h + 1) * size, :], p.astype(bf16))
                new.append((m_new, total, acc))
            return tuple(new)

        init = tuple(
            (
                jnp.full((1, q_tile), NEGATIVE, f32),
                jnp.zeros((1, q_tile), f32),
                jnp.zeros((size, q_tile), f32),
            )
            for _ in range(heads)
        )
        result = lax.fori_loop(k_lo, k_hi, body, init)
        mixed = jnp.concatenate([acc / total for _, total, acc in result], axis=0)
        cols = slice(t * q_tile, (t + 1) * q_tile)
        ot_ref[:, cols] = mixed
        for h, (m, total, _) in enumerate(result):
            log_ref[h : h + 1, cols] = m + jnp.log(total)
        os[cols, :] = mixed.T.astype(bf16)
    for i in range(blocks):
        ref, rows = block_rows(out_refs, i)
        ref[rows, :] = os[rows_at(info_ref[3 * blocks + i]), :]


def bwd_kernel(parts, heads, size, q_tile, key_tile, *refs):
    info_ref = refs[0]
    q_refs = refs[1 : 1 + parts]
    kv_refs = refs[1 + parts : 1 + 3 * parts]
    g_refs = refs[1 + 3 * parts : 1 + 4 * parts]
    ot_ref, log_ref = refs[1 + 4 * parts : 3 + 4 * parts]
    dq_refs = refs[3 + 4 * parts : 3 + 5 * parts]
    dkv_refs = refs[3 + 5 * parts : 3 + 7 * parts]
    ks, kt_s, vs, qs, gs, qtd, gtd, qd, gd, dk, dv, dqs = refs[3 + 7 * parts :]
    width = heads * size
    qn = qs.shape[0]
    blocks = qn // DEAL
    load_sorted(info_ref, kv_refs, width, blocks, ks, vs)
    for i in range(blocks):
        to = rows_at(info_ref[3 * blocks + i])
        ref, rows = block_rows(q_refs, i)
        qs[to, :] = ref[rows, :] * bf16(size**-0.5)
        ref, rows = block_rows(g_refs, i)
        gs[to, :] = ref[rows, :]
    kn = ks.shape[0]
    for t in range(kn // key_tile):
        kt_s[t] = ks[t * key_tile : (t + 1) * key_tile, :].T
    dk[...] = jnp.zeros_like(dk)
    dv[...] = jnp.zeros_like(dv)
    col = lax.broadcasted_iota(jnp.int32, (q_tile, width), 1) // size
    sub = lax.broadcasted_iota(jnp.int32, (key_tile, q_tile), 0)
    for t in range(qn // q_tile):
        cols = slice(t * q_tile, (t + 1) * q_tile)
        position, low, k_lo, k_hi = tile_bounds(info_ref, t, q_tile, key_tile, blocks)
        qtile = qs[cols, :]
        gtile = gs[cols, :]
        gt = gtile.T
        block_diag(qtile.T, qtd, heads, size, q_tile)
        block_diag(gt, gtd, heads, size, q_tile)
        for h in range(heads):
            hc = slice(h * q_tile, (h + 1) * q_tile)
            qd[hc, :] = jnp.where(col == h, qtile, jnp.zeros_like(qtile))
            gd[hc, :] = jnp.where(col == h, gtile, jnp.zeros_like(gtile))
        prod = gt.astype(f32) * ot_ref[:, cols]
        deltas = [
            jnp.sum(prod[h * size : (h + 1) * size], axis=0, keepdims=True) for h in range(heads)
        ]
        logs = [log_ref[h : h + 1, cols] for h in range(heads)]

        def body(k, carry):
            rows = pl.ds(pl.multiple_of(k * key_tile, key_tile), key_tile)
            kt = ks[rows, :]
            vtile = vs[rows, :]
            ktt = kt_s[k]
            kp = sub + k * key_tile
            ok = (kp <= position) & (kp >= low)
            new, probs, grads = [], [], []
            for h in range(heads):
                hc = slice(h * q_tile, (h + 1) * q_tile)
                s = dot(kt, qtd[:, hc])
                p = jnp.exp(jnp.where(ok, s, NEGATIVE) - logs[h])
                dp = dot(vtile, gtd[:, hc])
                ds = (p * (dp - deltas[h])).astype(bf16)
                new.append(carry[h] + dot(ktt[h * size : (h + 1) * size, :], ds))
                probs.append(p.astype(bf16))
                grads.append(ds)
            dv[rows, :] += dot(jnp.concatenate(probs, axis=1), gd[...])
            dk[rows, :] += dot(jnp.concatenate(grads, axis=1), qd[...])
            return tuple(new)

        result = lax.fori_loop(
            k_lo, k_hi, body, tuple(jnp.zeros((size, q_tile), f32) for _ in range(heads))
        )
        dqs[cols, :] = (jnp.concatenate(result, axis=0).T * (size**-0.5)).astype(bf16)
    for i in range(blocks):
        ref, rows = block_rows(dq_refs, i)
        ref[rows, :] = dqs[rows_at(info_ref[3 * blocks + i]), :]
    for i in range(2 * blocks):
        ref, rows = block_rows(dkv_refs, i)
        at = rows_at(info_ref[i])
        ref[rows, :width] = dk[at, :].astype(bf16)
        ref[rows, width:] = dv[at, :].astype(bf16)


def attn_fwd(info, q, kv, heads, size, q_tile=512, key_tile=512):
    parts = len(q)
    rows, w = q[0].shape
    n = parts * rows
    kn = 2 * n
    outs = pl.pallas_call(
        functools.partial(fwd_kernel, parts, heads, size, q_tile, key_tile),
        out_shape=tuple(jax.ShapeDtypeStruct((rows, w), bf16) for _ in range(parts))
        + (jax.ShapeDtypeStruct((w, n), f32), jax.ShapeDtypeStruct((heads, n), f32)),
        in_specs=[SM] + [VM] * (3 * parts),
        out_specs=(VM,) * (parts + 2),
        scratch_shapes=[
            pltpu.VMEM((kn, w), bf16),
            pltpu.VMEM((kn // key_tile, w, key_tile), bf16),
            pltpu.VMEM((kn, w), bf16),
            pltpu.VMEM((n, w), bf16),
            pltpu.VMEM((w, heads * q_tile), bf16),
            pltpu.VMEM((n, w), bf16),
        ],
        cost_estimate=pl.CostEstimate(
            flops=4 * n * kn * w, bytes_accessed=16 * n * w, transcendentals=n * kn * heads // 2
        ),
        compiler_params=pltpu.CompilerParams(vmem_limit_bytes=40 << 20),
        name="attn_fwd",
    )(info, *q, *kv)
    return outs[:parts], outs[parts], outs[parts + 1]


def attn_bwd(info, q, kv, g, ot, log, heads, size, q_tile=256, key_tile=512):
    parts = len(q)
    rows, w = q[0].shape
    n = parts * rows
    kn = 2 * n
    outs = pl.pallas_call(
        functools.partial(bwd_kernel, parts, heads, size, q_tile, key_tile),
        out_shape=tuple(jax.ShapeDtypeStruct((rows, w), bf16) for _ in range(parts))
        + tuple(jax.ShapeDtypeStruct((rows, 2 * w), bf16) for _ in range(2 * parts)),
        in_specs=[SM] + [VM] * (4 * parts + 2),
        out_specs=(VM,) * (3 * parts),
        scratch_shapes=[
            pltpu.VMEM((kn, w), bf16),
            pltpu.VMEM((kn // key_tile, w, key_tile), bf16),
            pltpu.VMEM((kn, w), bf16),
            pltpu.VMEM((n, w), bf16),
            pltpu.VMEM((n, w), bf16),
            pltpu.VMEM((w, heads * q_tile), bf16),
            pltpu.VMEM((w, heads * q_tile), bf16),
            pltpu.VMEM((heads * q_tile, w), bf16),
            pltpu.VMEM((heads * q_tile, w), bf16),
            pltpu.VMEM((kn, w), f32),
            pltpu.VMEM((kn, w), f32),
            pltpu.VMEM((n, w), bf16),
        ],
        cost_estimate=pl.CostEstimate(
            flops=10 * n * kn * w, bytes_accessed=32 * n * w, transcendentals=n * kn * heads // 2
        ),
        compiler_params=pltpu.CompilerParams(vmem_limit_bytes=50 << 20),
        name="attn_bwd",
    )(info, *q, *kv, *g, ot, log)
    return outs[:parts], outs[parts : 2 * parts], outs[2 * parts :]


def swap(x, axis, mask):
    return lax.ppermute(x, axis, [(i, i ^ mask) for i in range(lax.axis_size(axis))])


def gather_tp(own):
    near = swap(own, "tp", 2)
    first = jnp.concatenate([own, swap(own, "tp", 1)], axis=0)
    second = jnp.concatenate([near, swap(near, "tp", 1)], axis=0)
    return first, second


def scatter_tp(first, second):
    s = first.shape[0] // 2
    away = second[:s] + swap(second[s:].astype(bf16), "tp", 1).astype(f32)
    away = swap(away.astype(bf16), "tp", 2).astype(f32)
    here = first[:s] + swap(first[s:].astype(bf16), "tp", 1).astype(f32)
    return here + away


def norm_stats(source):
    center = jnp.mean(source, axis=-1, keepdims=True)
    offsets = source - center
    spread = jnp.mean(offsets * offsets, axis=-1, keepdims=True)
    inverse = lax.rsqrt(spread + EPSILON)
    return offsets * inverse, inverse


def norm_back(grad, normed, inverse, gain):
    scaled = grad * gain
    return (
        scaled
        - jnp.mean(scaled, axis=-1, keepdims=True)
        - normed * jnp.mean(scaled * normed, axis=-1, keepdims=True)
    ) * inverse


def gelu_and_slope(v):
    t = jnp.tanh(GELU_SCALE * (v + GELU_CUBIC * v * v * v))
    slope = 0.5 * (1.0 + t) + 0.5 * v * (1.0 - t * t) * GELU_SCALE * (
        1.0 + 3.0 * GELU_CUBIC * v * v
    )
    return 0.5 * v * (1.0 + t), slope


def shards(
    tokens,
    cotangent,
    lengths,
    deal,
    ln1_gain,
    ln1_bias,
    w_qkv,
    b_qv,
    w_out,
    b_out,
    ln2_gain,
    ln2_bias,
    w_fc,
    b_fc,
    w_proj,
    b_proj,
):
    micro_count, share, model = tokens.shape
    row_len = deal.shape[1]
    fsdp = lax.axis_size("fsdp")
    tp = lax.axis_size("tp")
    ctx_at = lax.axis_index("ctx")
    tp_at = lax.axis_index("tp")
    fsdp_at = lax.axis_index("fsdp")
    part = model // fsdp
    width = w_qkv.shape[2]
    heads = b_qv.shape[1]
    size = width // heads
    hidden = w_fc.shape[1]

    pieces = [ln1_gain, ln1_bias, b_out, ln2_gain, ln2_bias, b_proj, b_qv.reshape(-1), b_fc.reshape(-1)]
    small = lax.all_gather(jnp.concatenate(pieces), "fsdp", axis=0, tiled=False)
    gain_one, bias_one, out_bias, gain_two, bias_two, proj_bias = (
        small[:, i * part : (i + 1) * part].reshape(1, model).astype(f32) for i in range(6)
    )
    rest = small[:, 6 * part :]
    qv = rest[:, : b_qv.size].reshape(fsdp, 2, heads, size // fsdp)
    qv = qv.transpose(1, 2, 0, 3).reshape(2, 1, width).astype(f32)
    fc_bias = rest[:, b_qv.size :].reshape(fsdp, b_fc.shape[0], b_fc.shape[1])
    fc_bias = fc_bias.transpose(1, 0, 2).reshape(1, hidden).astype(f32)

    def gather(w):
        return lax.all_gather(w, "fsdp", axis=0, tiled=True)

    weight_qkv = gather(w_qkv.reshape(part, 3 * width))
    weight_q, weight_kv = weight_qkv[:, :width], weight_qkv[:, width:]
    weight_out = gather(w_out.T)
    weight_fc = gather(w_fc)
    weight_proj = gather(w_proj.T)

    per = share // DEAL
    table = (deal[:, ::DEAL] // DEAL).reshape(micro_count, 2, tp, per)
    order = tp_at ^ jnp.arange(tp)
    table = jnp.take(table, order, axis=2).reshape(micro_count, 2, tp * per)
    own = jnp.take(table, ctx_at, axis=1)
    other = jnp.take(table, 1 - ctx_at, axis=1)
    blocks = tp * per
    rank = jnp.sum((own[:, None, :] < own[:, :, None]).astype(jnp.int32), axis=2)
    ordered = jnp.sum(
        jnp.where(rank[:, :, None] == jnp.arange(blocks)[None, None], own[:, :, None], 0), axis=1
    )
    ends = jnp.cumsum(lengths, axis=1)
    info = jnp.concatenate([own, other, ordered, rank, ends], axis=1)
    own_slots = (ctx_at * tp + tp_at) * share
    own_positions = lax.dynamic_slice_in_dim(deal, own_slots, share, axis=1)

    states = []
    for r in range(micro_count):
        source = tokens[r].astype(f32)
        one, inverse_one = norm_stats(source)
        normed = gather_tp((one * gain_one + bias_one).astype(bf16))
        kv = [(dot(x, weight_kv) + jnp.concatenate([jnp.zeros_like(qv[1]), qv[1]], 1)).astype(bf16) for x in normed]
        kv_other = [swap(x, "ctx", 1) for x in kv]
        q = [(dot(x, weight_q) + qv[0]).astype(bf16) for x in normed]
        valid = (own_positions[r] < ends[r, -1])[:, None]
        out_grad = jnp.where(valid, cotangent[r], jnp.zeros_like(cotangent[r]))
        out_grads = gather_tp(out_grad)
        mixed, mixed_t, log = attn_fwd(info[r], q, kv + kv_other, heads, size)
        hidden_one = source + scatter_tp(*[dot_t(x, weight_out) for x in mixed]) + out_bias
        two, inverse_two = norm_stats(hidden_one)
        second = gather_tp((two * gain_two + bias_two).astype(bf16))
        before = [dot(x, weight_fc) + fc_bias for x in second]
        act = [gelu_and_slope(x)[0].astype(bf16) for x in before]
        layer_out = hidden_one + scatter_tp(*[dot_t(x, weight_proj) for x in act]) + proj_bias
        out_grad = out_grad.astype(f32)
        before_grad = [
            (dot(g, weight_proj) * gelu_and_slope(x)[1]).astype(bf16)
            for g, x in zip(out_grads, before)
        ]
        second_grad = scatter_tp(*[dot_t(x, weight_fc) for x in before_grad])
        hidden_grad = out_grad + norm_back(second_grad, two, inverse_two, gain_two)
        hidden_grads = gather_tp(hidden_grad.astype(bf16))
        mixed_grad = [dot(x, weight_out).astype(bf16) for x in hidden_grads]
        dq, dkv, dkv_other = attn_bwd(info[r], q, kv + kv_other, mixed_grad, mixed_t, log, heads, size)
        dkv = [
            (x.astype(f32) + swap(y, "ctx", 1).astype(f32)).astype(bf16)
            for x, y in zip(dkv, dkv_other)
        ]
        first_grad = scatter_tp(*[dot_t(x, weight_q) + dot_t(y, weight_kv) for x, y in zip(dq, dkv)])
        token_grad = hidden_grad + norm_back(first_grad, one, inverse_one, gain_one)
        vectors = jnp.concatenate(
            [
                jnp.sum(x, axis=0)
                for x in (
                    first_grad * one,
                    first_grad,
                    hidden_grad,
                    second_grad * two,
                    second_grad,
                    out_grad,
                )
            ]
        )
        shared = jnp.concatenate(
            [
                sum(jnp.sum(x.astype(f32), axis=0) for x in dq),
                sum(jnp.sum(x[:, width:].astype(f32), axis=0) for x in dkv),
                sum(jnp.sum(x.astype(f32), axis=0) for x in before_grad),
            ]
        )
        states.append(
            dict(
                layer_out=layer_out.astype(bf16),
                token_grad=token_grad,
                vectors=vectors,
                shared=shared,
                pairs=dict(
                    proj=list(zip(out_grads, act)),
                    fc=list(zip(second, before_grad)),
                    out=list(zip(hidden_grads, mixed)),
                    q=list(zip(normed, dq)),
                    kv=list(zip(normed, dkv)),
                ),
            )
        )

    def weight_grad(*names):
        whole = jnp.concatenate(
            [
                sum(t_dot(a, b) for s in states for a, b in s["pairs"][name]).astype(bf16)
                for name in names
            ],
            axis=1,
        )
        own_part = lax.psum_scatter(whole, "fsdp", scatter_dimension=0, tiled=True)
        return own_part.astype(f32) + swap(own_part, "ctx", 1).astype(f32)

    grad_proj = weight_grad("proj").T
    grad_fc = weight_grad("fc")
    grad_out = weight_grad("out").T
    grad_qkv = weight_grad("q", "kv").reshape(part, 3, width)

    vectors = lax.psum(sum(s["vectors"] for s in states), ("fsdp", "ctx", "tp"))
    vectors = vectors.reshape(6, fsdp, part)
    vectors = lax.dynamic_index_in_dim(vectors, fsdp_at, axis=1, keepdims=False)
    shared = lax.psum(sum(s["shared"] for s in states), ("fsdp", "ctx"))
    grad_qv = shared[: 2 * width].reshape(2, heads, fsdp, size // fsdp)
    grad_qv = lax.dynamic_index_in_dim(grad_qv, fsdp_at, axis=2, keepdims=False)
    grad_fc_bias = shared[2 * width :].reshape(b_fc.shape[0], fsdp, b_fc.shape[1])
    grad_fc_bias = lax.dynamic_index_in_dim(grad_fc_bias, fsdp_at, axis=1, keepdims=False)
    return (
        jnp.stack([s["layer_out"] for s in states]),
        jnp.stack([s["token_grad"] for s in states]),
        vectors[0],
        vectors[1],
        grad_qkv,
        grad_qv,
        grad_out,
        vectors[2],
        vectors[3],
        vectors[4],
        grad_fc,
        grad_fc_bias,
        grad_proj,
        vectors[5],
    )


def solution(mesh):
    in_specs = (
        P("fsdp", ("ctx", "tp"), None),
        P("fsdp", ("ctx", "tp"), None),
        P("fsdp", None),
        P("fsdp", None),
        P("fsdp"),
        P("fsdp"),
        P("fsdp", None, "tp"),
        P(None, "tp", "fsdp"),
        P("tp", "fsdp"),
        P("fsdp"),
        P("fsdp"),
        P("fsdp"),
        P("fsdp", "tp"),
        P("tp", "fsdp"),
        P("tp", "fsdp"),
        P("fsdp"),
    )
    out_specs = (
        P("fsdp", ("ctx", "tp"), None),
        P("fsdp", ("ctx", "tp"), None),
        P("fsdp"),
        P("fsdp"),
        P("fsdp", None, "tp"),
        P(None, "tp", "fsdp"),
        P("tp", "fsdp"),
        P("fsdp"),
        P("fsdp"),
        P("fsdp"),
        P("fsdp", "tp"),
        P("tp", "fsdp"),
        P("tp", "fsdp"),
        P("fsdp"),
    )
    return jax.shard_map(shards, mesh=mesh, in_specs=in_specs, out_specs=out_specs, check_vma=False)
```

time: 1370 us -> 561 us (0.41)
  waiting for transfers between devices: 710 us -> 149 us
  matrix products: 309 us -> 90.8 us
  other arithmetic: 155 us -> 44.2 us
  Pallas kernels: 0 us -> 66.2 us
  blocking collectives: 143 us -> 100 us
  starting transfers between devices: 3.46 us -> 41.9 us
  local copies, waits for them, and re-layouts: 24.3 us -> 43 us
    reduce_scatter x20 -> x4, waiting for transfers between devices: 442 us -> 0.05 us  [weight_grad(): own_part = lax.psum_scatter(whole, 'fsdp', scatter_dimension=0, tiled=True)]
    dot_general x36 -> x60, matrix products: 309 us -> 90.8 us  [the longest x20 37.9 us: t_dot(): lax.dot_general(a, b, (((0,), (0,)), ((), ())), preferred_element_type=f32)]
    all_gather x15 -> x3, waiting for transfers between devices: 215 us -> 9.07 us  [gather(): return lax.all_gather(w, 'fsdp', axis=0, tiled=True)]
    ppermute x0 -> x60, waiting for transfers between devices: none -> 140 us  [swap(): lax.ppermute(x, axis, [(i, i ^ mask) for i in range(lax.axis_size(axis))])]
    convert_element_type x26 -> x17, other arithmetic: 81.8 us -> 10.7 us  [the longest x8 6.16 us: scatter_tp(): away = swap(away.astype(bf16), 'tp', 2).astype(f32)]
    all_gather x9 -> x2, blocking collectives: 106 us -> 38.7 us  [the longest x1 23 us: gather(): return lax.all_gather(w, 'fsdp', axis=0, tiled=True)]
    pallas_call x0 -> x4, Pallas kernels: none -> 66.2 us  [the longest x2 38.4 us: attn_bwd(): pl.pallas_call(functools.partial(bwd_kernel, parts, heads, size, q_tile,...]
    reduce_sum x22 -> x20, other arithmetic: 61.3 us -> 17.3 us  [the longest x5 12.5 us: shards(): jnp.sum(x, axis=0)]
  transfers between devices with their start and end apart: 40 -> 67, of which waited for: 28 -> 21; matrix products, arithmetic and copies ran while one was open for 33% -> 29% of each run, Pallas kernels for 0% -> 12%
where the time goes in v1:
time: 561 us; the launch traced here: 552 us
  waiting for transfers between devices  149 us (27%)
  blocking collectives  100 us (18%)
  matrix products  90.8 us (16%)
  Pallas kernels  66.2 us (12%)
  other arithmetic  44.2 us (8%)
  local copies, waits for them, and re-layouts  43 us (8%)
  starting transfers between devices  41.9 us (7%)
  between operations  16.9 us (3%)
    ppermute x60, waiting for transfers between devices, swap(): lax.ppermute(x, axis, [(i, i ^ mask) for i in range(lax.axis_size(axis))])  140 us
    ppermute x60, starting transfers between devices, swap(): lax.ppermute(x, axis, [(i, i ^ mask) for i in range(lax.axis_size(axis))])  40.7 us
    pallas_call x2, Pallas kernels, attn_bwd(): pl.pallas_call(functools.partial(bwd_kernel, parts, heads, size, q_tile,...  38.4 us
    psum x1, blocking collectives, shards(): lax.psum(sum((s['vectors'] for s in states)), ('fsdp', 'ctx', 'tp'))  38.1 us
    dot_general x20, matrix products, t_dot(): lax.dot_general(a, b, (((0,), (0,)), ((), ())), preferred_element_type=f32)  37.9 us
    dot_general x20, matrix products, dot(): return jnp.dot(a, b, preferred_element_type=f32)  35 us
    pallas_call x2, Pallas kernels, attn_fwd(): pl.pallas_call(functools.partial(fwd_kernel, parts, heads, size, q_tile,...  27.8 us
    unnamed x237, local copies, waits for them, and re-layouts  26.4 us
  transfers between devices with their start and end apart: 67, of which 21 were waited for; matrix products, arithmetic and copies ran while one was open for 29% of the time, Pallas kernels for 12%

profile of v1, /device:TPU:0, one launch (start us, length us, event | category | flops | bytes accessed | tf_op | source)
XLA Modules:
  0.0 552.0 jit_solution(5922928203590787669)
XLA Ops:
  7.2 2.0 copy.51
  16.2 15.7 %all-gather.1 = bf16[4,1,1920]{2,1,0:T(2,128)(2,1)S(1)} all-gather(bf16[1,1,1920]{2,1,0:T(2,128)(2,1)S(1)} %reshape.380), channel_id=2, replica_groups=mesh['fsdp'=4,'ctx'=2,'tp'=4] {'fsdp'}, dimensions={0}, use_global_device_ids=true | all-gather | bytes 19200 | tf_op jit(solution)/shard_map/all_gather | solution.py:351
  37.2 2.1 compare_reduce_fusion.1
  39.3 2.0 convert_reduce_fusion.5
  45.1 4.1 collective-permute-done.1
  49.3 11.2 %collective-permute-done.15 = bf16[256,1024]{1,0:T(8,128)(2,1)} collective-permute-done((bf16[256,1024]{1,0:T(8,128)(2,1)}, bf16[256,1024]{1,0:T(8,128)(2,1)}, u32[]{:S(2)}, u32[]{:S(2)}) %collective-permute-start.15) | collective-permute-done | bytes 524320 | tf_op jit(solution)/shard_map/ppermute | solution.py:276
  60.5 23.0 %all_gather.21 = bf16[1024,256]{0,1:T(8,128)(2,1)} all-gather(bf16[256,256]{0,1:T(8,128)(2,1)S(1)} %bitcast.226), channel_id=1, replica_groups=mesh['fsdp'=4,'ctx'=2,'tp'=4] {'fsdp'}, dimensions={0}, use_global_device_ids=true | all-gather | bytes 655360 | tf_op jit(solution)/shard_map/all_gather | solution.py:362
  85.9 1.6 collective-permute-start.44
  90.1 2.7 fusion.34.refs_3_
  92.8 1.6 collective-permute-start.3
  96.6 1.8 fusion.36.refs_3_
  98.4 1.6 collective-permute-start.17
  100.5 1.6 fusion.52.refs_1_
  105.0 2.7 collective-permute-done.3.refs_5_
  109.2 9.7 %collective-permute-done.4.refs_6_ = bf16[512,512]{1,0:T(8,128)(2,1)S(1)} collective-permute-done((bf16[512,512]{1,0:T(8,128)(2,1)S(1)}, bf16[512,512]{1,0:T(8,128)(2,1)S(1)}, u32[]{:S(2)}, u32[]{:S(2)}) %collective-permute-start.4) | collective-permute-done | bytes 524320 | tf_op jit(solution)/shard_map/ppermute | solution.py:276
  119.0 14.0 %attn_fwd.2 = (bf16[512,256]{1,0:T(8,128)(2,1)S(1)}, bf16[512,256]{1,0:T(8,128)(2,1)S(1)}, f32[256,1024]{1,0:T(8,128)S(1)}, f32[4,1024]{1,0:T(4,128)S(1)}) custom-call(s32[66]{0:T(128)S(1)} %get-tuple-element.198.refs_0_, bf16[512,256]{1,0:T(8,128)(2,1)S(1)} %fusion.52.refs_1_, bf16[512,256]{1,0:T(8,128)(2,1)S(1)} %fusion.53.refs_2_, ...), custom_call_target="tpu_custom_call" | custom-call | flops 2147483648 | bytes 4194304 | tf_op jit(solution)/shard_map/attn_fwd/pallas_call | solution.py:218
  135.5 3.5 collective-permute-done.18.refs_6_
  139.0 13.8 %attn_fwd.3 = (bf16[512,256]{1,0:T(8,128)(2,1)S(1)}, bf16[512,256]{1,0:T(8,128)(2,1)S(1)}, f32[256,1024]{1,0:T(8,128)S(1)}, f32[4,1024]{1,0:T(4,128)S(1)}) custom-call(s32[66]{0:T(128)S(1)} %get-tuple-element.199.refs_0_, bf16[512,256]{1,0:T(8,128)(2,1)S(1)} %fusion.54.refs_1_, bf16[512,256]{1,0:T(8,128)(2,1)S(1)} %fusion.55.refs_2_, ...), custom_call_target="tpu_custom_call" | custom-call | flops 2147483648 | bytes 4194304 | tf_op jit(solution)/shard_map/attn_fwd/pallas_call | solution.py:218
  159.0 11.7 %collective-permute-done.7 = bf16[256,1024]{1,0:T(8,128)(2,1)} collective-permute-done((bf16[256,1024]{1,0:T(8,128)(2,1)}, bf16[256,1024]{1,0:T(8,128)(2,1)}, u32[]{:S(2)}, u32[]{:S(2)}) %collective-permute-start.7) | collective-permute-done | bytes 524320 | tf_op jit(solution)/shard_map/ppermute | solution.py:276
  170.6 10.3 %collective-permute-done.21 = bf16[256,1024]{1,0:T(8,128)(2,1)} collective-permute-done((bf16[256,1024]{1,0:T(8,128)(2,1)S(1)}, bf16[256,1024]{1,0:T(8,128)(2,1)}, u32[]{:S(2)}, u32[]{:S(2)}) %collective-permute-start.21) | collective-permute-done | bytes 524320 | tf_op jit(solution)/shard_map/ppermute | solution.py:276
  180.9 2.8 fusion.156
  193.3 4.5 fusion.105
  197.9 9.0 %all-gather.10.cloned.1.call-done = bf16[1024,1024]{0,1:T(8,128)(2,1)} async-done(((bf16[256,1024]{0,1:T(8,128)(2,1)}), bf16[1024,1024]{0,1:T(8,128)(2,1)}) %all-gather.10.cloned.1.call-update) | async-done | bytes 2097168 | tf_op jit(solution)/shard_map/all_gather | solution.py:362
  206.9 5.1 convert_reduce_fusion.3
  216.3 2.5 fusion.103
  218.8 3.6 convert_reduce_fusion.1
  230.5 2.4 convert_reduce_fusion.2
  238.2 2.4 convert_reduce_fusion
  248.3 12.2 %collective-permute-done.33 = bf16[256,1024]{1,0:T(8,128)(2,1)S(1)} collective-permute-done((bf16[256,1024]{1,0:T(8,128)(2,1)S(1)}, bf16[256,1024]{1,0:T(8,128)(2,1)S(1)}, u32[]{:S(2)}, u32[]{:S(2)}) %collective-permute-start.33) | collective-permute-done | bytes 524320 | tf_op jit(solution)/shard_map/ppermute | solution.py:276
  263.3 8.5 %collective-permute-done.13 = bf16[256,1024]{1,0:T(8,128)(2,1)S(1)} collective-permute-done((bf16[256,1024]{1,0:T(8,128)(2,1)S(1)}, bf16[256,1024]{1,0:T(8,128)(2,1)S(1)}, u32[]{:S(2)}, u32[]{:S(2)}) %collective-permute-start.13) | collective-permute-done | bytes 524320 | tf_op jit(solution)/shard_map/ppermute | solution.py:276
  271.8 11.2 %collective-permute-done.47 = bf16[256,1024]{1,0:T(8,128)(2,1)S(1)} collective-permute-done((bf16[256,1024]{1,0:T(8,128)(2,1)S(1)}, bf16[256,1024]{1,0:T(8,128)(2,1)S(1)}, u32[]{:S(2)}, u32[]{:S(2)}) %collective-permute-start.47) | collective-permute-done | bytes 524320 | tf_op jit(solution)/shard_map/ppermute | solution.py:276
  283.0 3.1 fusion.151
  286.1 7.3 %collective-permute-done.27 = bf16[256,1024]{1,0:T(8,128)(2,1)S(1)} collective-permute-done((bf16[256,1024]{1,0:T(8,128)(2,1)S(1)}, bf16[256,1024]{1,0:T(8,128)(2,1)S(1)}, u32[]{:S(2)}, u32[]{:S(2)}) %collective-permute-start.27) | collective-permute-done | bytes 524320 | tf_op jit(solution)/shard_map/ppermute | solution.py:276
  293.4 2.5 fusion.150
  298.3 4.6 fusion.99
  302.9 4.7 fusion.101
  307.6 14.0 %collective-permute-done.35 = bf16[256,1024]{1,0:T(8,128)(2,1)S(1)} collective-permute-done((bf16[256,1024]{1,0:T(8,128)(2,1)S(1)}, bf16[256,1024]{1,0:T(8,128)(2,1)S(1)}, u32[]{:S(2)}, u32[]{:S(2)}) %collective-permute-start.35) | collective-permute-done | bytes 524320 | tf_op jit(solution)/shard_map/ppermute | solution.py:276
  327.5 3.5 fusion.146
  332.6 3.3 add_convert_fusion
  336.0 2.9 fusion.102
  339.0 2.6 fusion.104
  343.2 2.8 add_convert_fusion.1
  347.1 2.2 pad_maximum_fusion.6
  352.1 18.3 %attn_bwd.2 = (bf16[512,256]{1,0:T(8,128)(2,1)S(1)}, bf16[512,256]{1,0:T(8,128)(2,1)S(1)}, bf16[512,512]{1,0:T(8,128)(2,1)S(1)}, bf16[512,512]{1,0:T(8,128)(2,1)...) custom-call(s32[66]{0:T(128)S(1)} %get-tuple-element.198.refs_0_, bf16[512,256]{1,0:T(8,128)(2,1)S(1)} %copy-done.13, ...), custom_call_target="tpu_custom_call" | custom-call | flops 5368709120 | bytes 8388608 | tf_op jit(solution)/shard_map/attn_bwd/pallas_call | solution.py:246
  370.5 5.3 collective-permute-start.39
  375.9 20.1 %attn_bwd.3 = (bf16[512,256]{1,0:T(8,128)(2,1)S(1)}, bf16[512,256]{1,0:T(8,128)(2,1)S(1)}, bf16[512,512]{1,0:T(8,128)(2,1)S(1)}, bf16[512,512]{1,0:T(8,128)(2,1)...) custom-call(s32[66]{0:T(128)S(1)} %get-tuple-element.199.refs_0_, bf16[512,256]{1,0:T(8,128)(2,1)S(1)} %copy-done.11, ...), custom_call_target="tpu_custom_call" | custom-call | flops 5368709120 | bytes 8388608 | tf_op jit(solution)/shard_map/attn_bwd/pallas_call | solution.py:246
  396.0 2.0 collective-permute-start.53
  398.5 1.6 fusion.142
  412.5 9.2 %collective-permute-done.51 = bf16[512,512]{1,0:T(8,128)(2,1)S(1)} collective-permute-done((bf16[512,512]{1,0:T(8,128)(2,1)S(1)}, bf16[512,512]{1,0:T(8,128)(2,1)S(1)}, u32[]{:S(2)}, u32[]{:S(2)}) %collective-permute-start.51) | collective-permute-done | bytes 524320 | tf_op jit(solution)/shard_map/ppermute | solution.py:276
  424.1 1.8 fusion.141
  425.9 1.8 fusion.143
  430.9 2.4 fusion.80
  435.0 2.0 fusion.76
  437.5 23.2 %psum.15 = f32[1536]{0:T(1024)S(1)} all-reduce(f32[1536]{0:T(1024)S(1)} %maximum_add_fusion), channel_id=1, replica_groups=mesh['fsdp'=4,'ctx'=2,'tp'=4] {'fsdp','ctx'}, use_global_device_ids=true, to_apply=%region_45.47 | all-reduce | flops 1536 | bytes 12288 | tf_op jit(solution)/shard_map/psum | solution.py:475
  462.3 3.9 collective-permute-done.57
  468.0 4.3 fusion.72
  472.4 38.1 %psum.14 = f32[6,4,256]{2,1,0:T(4,128)S(1)} all-reduce(f32[6,4,256]{2,1,0:T(4,128)S(1)} %reshape.303), channel_id=1, replica_groups=mesh['fsdp'=4,'ctx'=2,'tp'=4] {'fsdp','ctx','tp'}, use_global_device_ids=true, to_apply=%region_31.33 | all-reduce | flops 6144 | bytes 49152 | tf_op jit(solution)/shard_map/psum | solution.py:472
  510.6 2.3 collective-permute-start.59
  512.9 3.6 fusion.71
  517.1 3.2 pad_maximum_fusion
  520.3 2.0 collective-permute-start.56
  522.3 3.7 collective-permute-done.59
  528.5 8.6 %collective-permute-done.58 = bf16[256,1024]{1,0:T(8,128)(2,1)S(1)} collective-permute-done((bf16[256,1024]{1,0:T(8,128)(2,1)}, bf16[256,1024]{1,0:T(8,128)(2,1)S(1)}, u32[]{:S(2)}, u32[]{:S(2)}) %collective-permute-start.58) | collective-permute-done | bytes 524320 | tf_op jit(solution)/shard_map/ppermute | solution.py:276
  538.3 5.2 collective-permute-done.56
  (517 shorter events, 118.0 us)
Async XLA Ops:
  7.2 82.9 %all-gather.6.cloned.1.call-start = ((), (), s32[]{:S(2)}) async-start(), calls=%async_computation.4 | async-start | bytes 1966080 | tf_op jit(solution)/shard_map/all_gather | solution.py:362
  9.3 184.1 %all-gather.8.cloned.1.call-start = ((), (), s32[]{:S(2)}) async-start(), calls=%async_computation.5 | async-start | bytes 2621440 | tf_op jit(solution)/shard_map/all_gather | solution.py:362
  34.2 55.9 %collective-permute-start = (bf16[256,1024]{1,0:T(8,128)(2,1)}, bf16[256,1024]{1,0:T(8,128)(2,1)S(1)}, u32[]{:S(2)}, u32[]{:S(2)}) collective-permute-start(bf16[256,1024]{1,0:T(8,128)(2,1)} %get-tuple-element.162), channel_id=1, source_target_pairs={{0,1},{1,0},{2,3},{3,2},{4,5},{5,4},{6,7},{7,6},{8,9},{9,8},{10,11... | collective-permute-start | bytes 1572872 | tf_op jit(solution)/shard_map/ppermute | solution.py:276
  34.2 15.1 %collective-permute-start.1 = (bf16[256,1024]{1,0:T(8,128)(2,1)}, bf16[256,1024]{1,0:T(8,128)(2,1)}, u32[]{:S(2)}, u32[]{:S(2)}) collective-permute-start(bf16[256,1024]{1,0:T(8,128)(2,1)} %get-tuple-element.162), channel_id=1, source_target_pairs={{0,2},{1,3},{2,0},{3,1},{4,6},{5,7},{6,4},{7,5},{8,10},{9,11},{10,... | collective-permute-start | bytes 1572872 | tf_op jit(solution)/shard_map/ppermute | solution.py:276
  35.6 60.2 %collective-permute-start.14 = (bf16[256,1024]{1,0:T(8,128)(2,1)}, bf16[256,1024]{1,0:T(8,128)(2,1)S(1)}, u32[]{:S(2)}, u32[]{:S(2)}) collective-permute-start(bf16[256,1024]{1,0:T(8,128)(2,1)} %get-tuple-element.163), channel_id=1, source_target_pairs={{0,1},{1,0},{2,3},{3,2},{4,5},{5,4},{6,7},{7,6},{8,9},{9,8},{10,11... | collective-permute-start | bytes 1572872 | tf_op jit(solution)/shard_map/ppermute | solution.py:276
  35.8 24.7 %collective-permute-start.15 = (bf16[256,1024]{1,0:T(8,128)(2,1)}, bf16[256,1024]{1,0:T(8,128)(2,1)}, u32[]{:S(2)}, u32[]{:S(2)}) collective-permute-start(bf16[256,1024]{1,0:T(8,128)(2,1)} %get-tuple-element.163), channel_id=1, source_target_pairs={{0,2},{1,3},{2,0},{3,1},{4,6},{5,7},{6,4},{7,5},{8,10},{9,11},{10,... | collective-permute-start | bytes 1572872 | tf_op jit(solution)/shard_map/ppermute | solution.py:276
  41.3 115.0 %collective-permute-start.30 = (bf16[256,1024]{1,0:T(8,128)(2,1)}, bf16[256,1024]{1,0:T(8,128)(2,1)}, u32[]{:S(2)}, u32[]{:S(2)}) collective-permute-start(bf16[256,1024]{1,0:T(8,128)(2,1)} %get-tuple-element.151), channel_id=1, source_target_pairs={{0,2},{1,3},{2,0},{3,1},{4,6},{5,7},{6,4},{7,5},{8,10},{9,11},{10,... | collective-permute-start | bytes 1572872 | tf_op jit(solution)/shard_map/ppermute | solution.py:276
  42.7 164.2 %all-gather.10.cloned.1.call-start = ((), (), s32[]{:S(2)}) async-start(), calls=%async_computation.6 | async-start | bytes 2621440 | tf_op jit(solution)/shard_map/all_gather | solution.py:362
  49.3 36.6 %collective-permute-start.2 = (bf16[256,1024]{1,0:T(8,128)(2,1)}, bf16[256,1024]{1,0:T(8,128)(2,1)}, u32[]{:S(2)}, u32[]{:S(2)}) collective-permute-start(bf16[256,1024]{1,0:T(8,128)(2,1)} %collective-permute-done.1), channel_id=1, source_target_pairs={{0,1},{1,0},{2,3},{3,2},{4,5},{5,4},{6,7},{7,6},{8,9},{9,8},{10,11... | collective-permute-start | bytes 1572872 | tf_op jit(solution)/shard_map/ppermute | solution.py:276
  60.5 28.1 %collective-permute-start.16 = (bf16[256,1024]{1,0:T(8,128)(2,1)}, bf16[256,1024]{1,0:T(8,128)(2,1)}, u32[]{:S(2)}, u32[]{:S(2)}) collective-permute-start(bf16[256,1024]{1,0:T(8,128)(2,1)} %collective-permute-done.15), channel_id=1, source_target_pairs={{0,1},{1,0},{2,3},{3,2},{4,5},{5,4},{6,7},{7,6},{8,9},{9,8},{10,11... | collective-permute-start | bytes 1572872 | tf_op jit(solution)/shard_map/ppermute | solution.py:276
  85.9 72.5 %collective-permute-start.44 = (bf16[256,1024]{1,0:T(8,128)(2,1)}, bf16[256,1024]{1,0:T(8,128)(2,1)}, u32[]{:S(2)}, u32[]{:S(2)}) collective-permute-start(bf16[256,1024]{1,0:T(8,128)(2,1)} %get-tuple-element.170), channel_id=1, source_target_pairs={{0,2},{1,3},{2,0},{3,1},{4,6},{5,7},{6,4},{7,5},{8,10},{9,11},{10,... | collective-permute-start | bytes 1572872 | tf_op jit(solution)/shard_map/ppermute | solution.py:276
  92.8 14.9 %collective-permute-start.3 = (bf16[512,512]{1,0:T(8,128)(2,1)S(1)}, bf16[512,512]{1,0:T(8,128)(2,1)S(1)}, u32[]{:S(2)}, u32[]{:S(2)}) collective-permute-start(bf16[512,512]{1,0:T(8,128)(2,1)S(1)} %fusion.34.refs_3_), channel_id=1, source_target_pairs={{0,4},{4,0},{1,5},{5,1},{2,6},{6,2},{3,7},{7,3},{8,12},{12,8},{9,1... | collective-permute-start | bytes 1572872 | tf_op jit(solution)/shard_map/ppermute | solution.py:276
  95.2 23.7 %collective-permute-start.4 = (bf16[512,512]{1,0:T(8,128)(2,1)S(1)}, bf16[512,512]{1,0:T(8,128)(2,1)S(1)}, u32[]{:S(2)}, u32[]{:S(2)}) collective-permute-start(bf16[512,512]{1,0:T(8,128)(2,1)S(1)} %fusion.35.refs_4_), channel_id=1, source_target_pairs={{0,4},{4,0},{1,5},{5,1},{2,6},{6,2},{3,7},{7,3},{8,12},{12,8},{9,1... | collective-permute-start | bytes 1572872 | tf_op jit(solution)/shard_map/ppermute | solution.py:276
  98.4 36.6 %collective-permute-start.17 = (bf16[512,512]{1,0:T(8,128)(2,1)S(1)}, bf16[512,512]{1,0:T(8,128)(2,1)S(1)}, u32[]{:S(2)}, u32[]{:S(2)}) collective-permute-start(bf16[512,512]{1,0:T(8,128)(2,1)S(1)} %fusion.36.refs_3_), channel_id=1, source_target_pairs={{0,4},{4,0},{1,5},{5,1},{2,6},{6,2},{3,7},{7,3},{8,12},{12,8},{9,1... | collective-permute-start | bytes 1572872 | tf_op jit(solution)/shard_map/ppermute | solution.py:276
  107.7 31.3 %collective-permute-start.18 = (bf16[512,512]{1,0:T(8,128)(2,1)S(1)}, bf16[512,512]{1,0:T(8,128)(2,1)S(1)}, u32[]{:S(2)}, u32[]{:S(2)}) collective-permute-start(bf16[512,512]{1,0:T(8,128)(2,1)S(1)} %fusion.37.refs_4_), channel_id=1, source_target_pairs={{0,4},{4,0},{1,5},{5,1},{2,6},{6,2},{3,7},{7,3},{8,12},{12,8},{9,1... | collective-permute-start | bytes 1572872 | tf_op jit(solution)/shard_map/ppermute | solution.py:276
  133.5 20.5 %collective-permute-start.6 = (bf16[256,1024]{1,0:T(8,128)(2,1)S(1)}, bf16[256,1024]{1,0:T(8,128)(2,1)S(1)}, u32[]{:S(2)}, u32[]{:S(2)}) collective-permute-start(bf16[256,1024]{1,0:T(8,128)(2,1)S(1)} %slice.540), channel_id=1, source_target_pairs={{0,1},{1,0},{2,3},{3,2},{4,5},{5,4},{6,7},{7,6},{8,9},{9,8},{10,11... | collective-permute-start | bytes 1572872 | tf_op jit(solution)/shard_map/ppermute | solution.py:276
  135.0 23.4 %collective-permute-start.5 = (bf16[256,1024]{1,0:T(8,128)(2,1)}, bf16[256,1024]{1,0:T(8,128)(2,1)}, u32[]{:S(2)}, u32[]{:S(2)}) collective-permute-start(bf16[256,1024]{1,0:T(8,128)(2,1)} %slice.541), channel_id=1, source_target_pairs={{0,1},{1,0},{2,3},{3,2},{4,5},{5,4},{6,7},{7,6},{8,9},{9,8},{10,11... | collective-permute-start | bytes 1572872 | tf_op jit(solution)/shard_map/ppermute | solution.py:276
  154.0 4.9 collective-permute-start.19
  155.5 15.1 %collective-permute-start.7 = (bf16[256,1024]{1,0:T(8,128)(2,1)}, bf16[256,1024]{1,0:T(8,128)(2,1)}, u32[]{:S(2)}, u32[]{:S(2)}) collective-permute-start(bf16[256,1024]{1,0:T(8,128)(2,1)} %fusion.96), channel_id=1, source_target_pairs={{0,2},{1,3},{2,0},{3,1},{4,6},{5,7},{6,4},{7,5},{8,10},{9,11},{10,... | collective-permute-start | bytes 1572872 | tf_op jit(solution)/shard_map/ppermute | solution.py:276
  156.3 24.7 %collective-permute-start.21 = (bf16[256,1024]{1,0:T(8,128)(2,1)S(1)}, bf16[256,1024]{1,0:T(8,128)(2,1)}, u32[]{:S(2)}, u32[]{:S(2)}) collective-permute-start(bf16[256,1024]{1,0:T(8,128)(2,1)S(1)} %fusion.89), channel_id=1, source_target_pairs={{0,2},{1,3},{2,0},{3,1},{4,6},{5,7},{6,4},{7,5},{8,10},{9,11},{10,... | collective-permute-start | bytes 1572872 | tf_op jit(solution)/shard_map/ppermute | solution.py:276
  157.8 303.0 %reduce-scatter.7.cloned.1.call-start = ((), (), s32[]{:S(2)}) async-start(), calls=%async_computation.8 | async-start | bytes 655360 | tf_op jit(solution)/shard_map/reduce_scatter | solution.py:464
  158.4 30.3 %collective-permute-start.31 = (bf16[256,1024]{1,0:T(8,128)(2,1)}, bf16[256,1024]{1,0:T(8,128)(2,1)}, u32[]{:S(2)}, u32[]{:S(2)}) collective-permute-start(bf16[256,1024]{1,0:T(8,128)(2,1)} %collective-permute-done.30), channel_id=1, source_target_pairs={{0,1},{1,0},{2,3},{3,2},{4,5},{5,4},{6,7},{7,6},{8,9},{9,8},{10,11... | collective-permute-start | bytes 1572872 | tf_op jit(solution)/shard_map/ppermute | solution.py:276
  158.5 31.3 %collective-permute-start.45 = (bf16[256,1024]{1,0:T(8,128)(2,1)}, bf16[256,1024]{1,0:T(8,128)(2,1)}, u32[]{:S(2)}, u32[]{:S(2)}) collective-permute-start(bf16[256,1024]{1,0:T(8,128)(2,1)} %collective-permute-done.44), channel_id=1, source_target_pairs={{0,1},{1,0},{2,3},{3,2},{4,5},{5,4},{6,7},{7,6},{8,9},{9,8},{10,11... | collective-permute-start | bytes 1572872 | tf_op jit(solution)/shard_map/ppermute | solution.py:276
  185.7 7.6 %collective-permute-start.8 = (bf16[256,1024]{1,0:T(8,128)(2,1)}, bf16[256,1024]{1,0:T(8,128)(2,1)}, u32[]{:S(2)}, u32[]{:S(2)}) collective-permute-start(bf16[256,1024]{1,0:T(8,128)(2,1)} %get-tuple-element.187), channel_id=1, source_target_pairs={{0,1},{1,0},{2,3},{3,2},{4,5},{5,4},{6,7},{7,6},{8,9},{9,8},{10,11... | collective-permute-start | bytes 1572872 | tf_op jit(solution)/shard_map/ppermute | solution.py:276
  185.7 12.2 %collective-permute-start.28 = (bf16[256,1024]{1,0:T(8,128)(2,1)}, bf16[256,1024]{1,0:T(8,128)(2,1)}, u32[]{:S(2)}, u32[]{:S(2)}) collective-permute-start(bf16[256,1024]{1,0:T(8,128)(2,1)} %get-tuple-element.151), channel_id=1, source_target_pairs={{0,1},{1,0},{2,3},{3,2},{4,5},{5,4},{6,7},{7,6},{8,9},{9,8},{10,11... | collective-permute-start | bytes 1572872 | tf_op jit(solution)/shard_map/ppermute | solution.py:276
  186.2 32.6 %collective-permute-start.42 = (bf16[256,1024]{1,0:T(8,128)(2,1)}, bf16[256,1024]{1,0:T(8,128)(2,1)}, u32[]{:S(2)}, u32[]{:S(2)}) collective-permute-start(bf16[256,1024]{1,0:T(8,128)(2,1)} %get-tuple-element.170), channel_id=1, source_target_pairs={{0,1},{1,0},{2,3},{3,2},{4,5},{5,4},{6,7},{7,6},{8,9},{9,8},{10,11... | collective-permute-start | bytes 1572872 | tf_op jit(solution)/shard_map/ppermute | solution.py:276
  191.2 33.3 %collective-permute-start.10 = (bf16[256,1024]{1,0:T(8,128)(2,1)}, bf16[256,1024]{1,0:T(8,128)(2,1)}, u32[]{:S(2)}, u32[]{:S(2)}) collective-permute-start(bf16[256,1024]{1,0:T(8,128)(2,1)} %get-tuple-element.187), channel_id=1, source_target_pairs={{0,2},{1,3},{2,0},{3,1},{4,6},{5,7},{6,4},{7,5},{8,10},{9,11},{10,... | collective-permute-start | bytes 1572872 | tf_op jit(solution)/shard_map/ppermute | solution.py:276
  191.9 34.3 %collective-permute-start.24 = (bf16[256,1024]{1,0:T(8,128)(2,1)}, bf16[256,1024]{1,0:T(8,128)(2,1)}, u32[]{:S(2)}, u32[]{:S(2)}) collective-permute-start(bf16[256,1024]{1,0:T(8,128)(2,1)} %get-tuple-element.188), channel_id=1, source_target_pairs={{0,2},{1,3},{2,0},{3,1},{4,6},{5,7},{6,4},{7,5},{8,10},{9,11},{10,... | collective-permute-start | bytes 1572872 | tf_op jit(solution)/shard_map/ppermute | solution.py:276
  193.3 22.9 %collective-permute-start.22 = (bf16[256,1024]{1,0:T(8,128)(2,1)}, bf16[256,1024]{1,0:T(8,128)(2,1)}, u32[]{:S(2)}, u32[]{:S(2)}) collective-permute-start(bf16[256,1024]{1,0:T(8,128)(2,1)} %get-tuple-element.188), channel_id=1, source_target_pairs={{0,1},{1,0},{2,3},{3,2},{4,5},{5,4},{6,7},{7,6},{8,9},{9,8},{10,11... | collective-permute-start | bytes 1572872 | tf_op jit(solution)/shard_map/ppermute | solution.py:276
  213.4 34.2 %collective-permute-start.29 = (bf16[256,1024]{1,0:T(8,128)(2,1)S(1)}, bf16[256,1024]{1,0:T(8,128)(2,1)S(1)}, u32[]{:S(2)}, u32[]{:S(2)}) collective-permute-start(bf16[256,1024]{1,0:T(8,128)(2,1)S(1)} %slice.533), channel_id=1, source_target_pairs={{0,1},{1,0},{2,3},{3,2},{4,5},{5,4},{6,7},{7,6},{8,9},{9,8},{10,11... | collective-permute-start | bytes 1572872 | tf_op jit(solution)/shard_map/ppermute | solution.py:276
  216.2 46.4 %collective-permute-start.9 = (bf16[256,1024]{1,0:T(8,128)(2,1)S(1)}, bf16[256,1024]{1,0:T(8,128)(2,1)S(1)}, u32[]{:S(2)}, u32[]{:S(2)}) collective-permute-start(bf16[256,1024]{1,0:T(8,128)(2,1)S(1)} %slice.539), channel_id=1, source_target_pairs={{0,1},{1,0},{2,3},{3,2},{4,5},{5,4},{6,7},{7,6},{8,9},{9,8},{10,11... | collective-permute-start | bytes 1572872 | tf_op jit(solution)/shard_map/ppermute | solution.py:276
  224.0 39.3 %collective-permute-start.43 = (bf16[256,1024]{1,0:T(8,128)(2,1)S(1)}, bf16[256,1024]{1,0:T(8,128)(2,1)S(1)}, u32[]{:S(2)}, u32[]{:S(2)}) collective-permute-start(bf16[256,1024]{1,0:T(8,128)(2,1)S(1)} %slice.529), channel_id=1, source_target_pairs={{0,1},{1,0},{2,3},{3,2},{4,5},{5,4},{6,7},{7,6},{8,9},{9,8},{10,11... | collective-permute-start | bytes 1572872 | tf_op jit(solution)/shard_map/ppermute | solution.py:276
  224.5 4.3 collective-permute-start.11
  226.2 9.8 %collective-permute-start.25 = (bf16[256,1024]{1,0:T(8,128)(2,1)}, bf16[256,1024]{1,0:T(8,128)(2,1)S(1)}, u32[]{:S(2)}, u32[]{:S(2)}) collective-permute-start(bf16[256,1024]{1,0:T(8,128)(2,1)} %collective-permute-done.24), channel_id=1, source_target_pairs={{0,1},{1,0},{2,3},{3,2},{4,5},{5,4},{6,7},{7,6},{8,9},{9,8},{10,11... | collective-permute-start | bytes 1572872 | tf_op jit(solution)/shard_map/ppermute | solution.py:276
  234.3 9.4 %collective-permute-start.32 = (bf16[256,1024]{1,0:T(8,128)(2,1)S(1)}, bf16[256,1024]{1,0:T(8,128)(2,1)S(1)}, u32[]{:S(2)}, u32[]{:S(2)}) collective-permute-start(bf16[256,1024]{1,0:T(8,128)(2,1)S(1)} %slice.532), channel_id=1, source_target_pairs={{0,1},{1,0},{2,3},{3,2},{4,5},{5,4},{6,7},{7,6},{8,9},{9,8},{10,11... | collective-permute-start | bytes 1572872 | tf_op jit(solution)/shard_map/ppermute | solution.py:276
  236.0 8.0 %collective-permute-start.12 = (bf16[256,1024]{1,0:T(8,128)(2,1)S(1)}, bf16[256,1024]{1,0:T(8,128)(2,1)S(1)}, u32[]{:S(2)}, u32[]{:S(2)}) collective-permute-start(bf16[256,1024]{1,0:T(8,128)(2,1)S(1)} %slice.538), channel_id=1, source_target_pairs={{0,1},{1,0},{2,3},{3,2},{4,5},{5,4},{6,7},{7,6},{8,9},{9,8},{10,11... | collective-permute-start | bytes 1572872 | tf_op jit(solution)/shard_map/ppermute | solution.py:276
  244.1 3.3 collective-permute-start.26
  245.7 14.8 %collective-permute-start.33 = (bf16[256,1024]{1,0:T(8,128)(2,1)S(1)}, bf16[256,1024]{1,0:T(8,128)(2,1)S(1)}, u32[]{:S(2)}, u32[]{:S(2)}) collective-permute-start(bf16[256,1024]{1,0:T(8,128)(2,1)S(1)} %fusion.82), channel_id=1, source_target_pairs={{0,2},{1,3},{2,0},{3,1},{4,6},{5,7},{6,4},{7,5},{8,10},{9,11},{10,... | collective-permute-start | bytes 1572872 | tf_op jit(solution)/shard_map/ppermute | solution.py:276
  247.4 38.8 %collective-permute-start.23 = (bf16[256,1024]{1,0:T(8,128)(2,1)S(1)}, bf16[256,1024]{1,0:T(8,128)(2,1)S(1)}, u32[]{:S(2)}, u32[]{:S(2)}) collective-permute-start(bf16[256,1024]{1,0:T(8,128)(2,1)S(1)} %slice.535), channel_id=1, source_target_pairs={{0,1},{1,0},{2,3},{3,2},{4,5},{5,4},{6,7},{7,6},{8,9},{9,8},{10,11... | collective-permute-start | bytes 1572872 | tf_op jit(solution)/shard_map/ppermute | solution.py:276
  247.6 24.1 %collective-permute-start.13 = (bf16[256,1024]{1,0:T(8,128)(2,1)S(1)}, bf16[256,1024]{1,0:T(8,128)(2,1)S(1)}, u32[]{:S(2)}, u32[]{:S(2)}) collective-permute-start(bf16[256,1024]{1,0:T(8,128)(2,1)S(1)} %fusion.91), channel_id=1, source_target_pairs={{0,2},{1,3},{2,0},{3,1},{4,6},{5,7},{6,4},{7,5},{8,10},{9,11},{10,... | collective-permute-start | bytes 1572872 | tf_op jit(solution)/shard_map/ppermute | solution.py:276
  260.5 22.5 %collective-permute-start.47 = (bf16[256,1024]{1,0:T(8,128)(2,1)S(1)}, bf16[256,1024]{1,0:T(8,128)(2,1)S(1)}, u32[]{:S(2)}, u32[]{:S(2)}) collective-permute-start(bf16[256,1024]{1,0:T(8,128)(2,1)S(1)} %fusion.78), channel_id=1, source_target_pairs={{0,2},{1,3},{2,0},{3,1},{4,6},{5,7},{6,4},{7,5},{8,10},{9,11},{10,... | collective-permute-start | bytes 1572872 | tf_op jit(solution)/shard_map/ppermute | solution.py:276
  262.7 30.7 %collective-permute-start.27 = (bf16[256,1024]{1,0:T(8,128)(2,1)S(1)}, bf16[256,1024]{1,0:T(8,128)(2,1)S(1)}, u32[]{:S(2)}, u32[]{:S(2)}) collective-permute-start(bf16[256,1024]{1,0:T(8,128)(2,1)S(1)} %fusion.84), channel_id=1, source_target_pairs={{0,2},{1,3},{2,0},{3,1},{4,6},{5,7},{6,4},{7,5},{8,10},{9,11},{10,... | collective-permute-start | bytes 1572872 | tf_op jit(solution)/shard_map/ppermute | solution.py:276
  296.0 26.2 %collective-permute-start.48 = (bf16[256,1024]{1,0:T(8,128)(2,1)S(1)}, bf16[256,1024]{1,0:T(8,128)(2,1)S(1)}, u32[]{:S(2)}, u32[]{:S(2)}) collective-permute-start(bf16[256,1024]{1,0:T(8,128)(2,1)S(1)} %convert_element_type.514), channel_id=1, source_target_pairs={{0,1},{1,0},{2,3},{3,2},{4,5},{5,4},{6,7},{7,6},{8,9},{9,8},{10,11... | collective-permute-start | bytes 1572872 | tf_op jit(solution)/shard_map/ppermute | solution.py:276
  296.1 25.6 %collective-permute-start.49 = (bf16[256,1024]{1,0:T(8,128)(2,1)S(1)}, bf16[256,1024]{1,0:T(8,128)(2,1)S(1)}, u32[]{:S(2)}, u32[]{:S(2)}) collective-permute-start(bf16[256,1024]{1,0:T(8,128)(2,1)S(1)} %convert_element_type.514), channel_id=1, source_target_pairs={{0,2},{1,3},{2,0},{3,1},{4,6},{5,7},{6,4},{7,5},{8,10},{9,11},{10,... | collective-permute-start | bytes 1572872 | tf_op jit(solution)/shard_map/ppermute | solution.py:276
  297.7 23.9 %collective-permute-start.35 = (bf16[256,1024]{1,0:T(8,128)(2,1)S(1)}, bf16[256,1024]{1,0:T(8,128)(2,1)S(1)}, u32[]{:S(2)}, u32[]{:S(2)}) collective-permute-start(bf16[256,1024]{1,0:T(8,128)(2,1)S(1)} %convert_element_type.494), channel_id=1, source_target_pairs={{0,2},{1,3},{2,0},{3,1},{4,6},{5,7},{6,4},{7,5},{8,10},{9,11},{10,... | collective-permute-start | bytes 1572872 | tf_op jit(solution)/shard_map/ppermute | solution.py:276
  302.9 19.7 %collective-permute-start.34 = (bf16[256,1024]{1,0:T(8,128)(2,1)S(1)}, bf16[256,1024]{1,0:T(8,128)(2,1)S(1)}, u32[]{:S(2)}, u32[]{:S(2)}) collective-permute-start(bf16[256,1024]{1,0:T(8,128)(2,1)S(1)} %convert_element_type.494), channel_id=1, source_target_pairs={{0,1},{1,0},{2,3},{3,2},{4,5},{5,4},{6,7},{7,6},{8,9},{9,8},{10,11... | collective-permute-start | bytes 1572872 | tf_op jit(solution)/shard_map/ppermute | solution.py:276
  321.6 2.9 collective-permute-start.50
  327.0 183.6 %reduce-scatter.11.cloned.1.call-start = ((), (), s32[]{:S(2)}) async-start(), calls=%async_computation.10 | async-start | bytes 2621440 | tf_op jit(solution)/shard_map/reduce_scatter | solution.py:464
  335.9 180.6 %reduce-scatter.9.cloned.1.call-start = ((), (), s32[]{:S(2)}) async-start(), calls=%async_computation.9 | async-start | bytes 2621440 | tf_op jit(solution)/shard_map/reduce_scatter | solution.py:464
  346.1 174.2 %reduce-scatter.5.cloned.1.call-start = ((), (), s32[]{:S(2)}) async-start(), calls=%async_computation.7 | async-start | bytes 1966080 | tf_op jit(solution)/shard_map/reduce_scatter | solution.py:464
  370.5 32.9 %collective-permute-start.39 = (bf16[512,512]{1,0:T(8,128)(2,1)S(1)}, bf16[512,512]{1,0:T(8,128)(2,1)}, u32[]{:S(2)}, u32[]{:S(2)}) collective-permute-start(bf16[512,512]{1,0:T(8,128)(2,1)S(1)} %get-tuple-element.46), channel_id=1, source_target_pairs={{0,4},{4,0},{1,5},{5,1},{2,6},{6,2},{3,7},{7,3},{8,12},{12,8},{9,1... | collective-permute-start | bytes 1572872 | tf_op jit(solution)/shard_map/ppermute | solution.py:276
  375.8 31.0 %collective-permute-start.37 = (bf16[512,512]{1,0:T(8,128)(2,1)S(1)}, bf16[512,512]{1,0:T(8,128)(2,1)S(1)}, u32[]{:S(2)}, u32[]{:S(2)}) collective-permute-start(bf16[512,512]{1,0:T(8,128)(2,1)S(1)} %get-tuple-element.43), channel_id=1, source_target_pairs={{0,4},{4,0},{1,5},{5,1},{2,6},{6,2},{3,7},{7,3},{8,12},{12,8},{9,1... | collective-permute-start | bytes 1572872 | tf_op jit(solution)/shard_map/ppermute | solution.py:276
  396.0 15.1 %collective-permute-start.53 = (bf16[512,512]{1,0:T(8,128)(2,1)S(1)}, bf16[512,512]{1,0:T(8,128)(2,1)S(1)}, u32[]{:S(2)}, u32[]{:S(2)}) collective-permute-start(bf16[512,512]{1,0:T(8,128)(2,1)S(1)} %get-tuple-element.54), channel_id=1, source_target_pairs={{0,4},{4,0},{1,5},{5,1},{2,6},{6,2},{3,7},{7,3},{8,12},{12,8},{9,1... | collective-permute-start | bytes 1572872 | tf_op jit(solution)/shard_map/ppermute | solution.py:276
  398.0 23.7 %collective-permute-start.51 = (bf16[512,512]{1,0:T(8,128)(2,1)S(1)}, bf16[512,512]{1,0:T(8,128)(2,1)S(1)}, u32[]{:S(2)}, u32[]{:S(2)}) collective-permute-start(bf16[512,512]{1,0:T(8,128)(2,1)S(1)} %get-tuple-element.51), channel_id=1, source_target_pairs={{0,4},{4,0},{1,5},{5,1},{2,6},{6,2},{3,7},{7,3},{8,12},{12,8},{9,1... | collective-permute-start | bytes 1572872 | tf_op jit(solution)/shard_map/ppermute | solution.py:276
  406.8 24.2 %collective-permute-start.40 = (bf16[256,1024]{1,0:T(8,128)(2,1)}, bf16[256,1024]{1,0:T(8,128)(2,1)}, u32[]{:S(2)}, u32[]{:S(2)}) collective-permute-start(bf16[256,1024]{1,0:T(8,128)(2,1)} %slice.530), channel_id=1, source_target_pairs={{0,1},{1,0},{2,3},{3,2},{4,5},{5,4},{6,7},{7,6},{8,9},{9,8},{10,11... | collective-permute-start | bytes 1572872 | tf_op jit(solution)/shard_map/ppermute | solution.py:276
  409.6 58.3 %collective-permute-start.38 = (bf16[256,1024]{1,0:T(8,128)(2,1)}, bf16[256,1024]{1,0:T(8,128)(2,1)}, u32[]{:S(2)}, u32[]{:S(2)}) collective-permute-start(bf16[256,1024]{1,0:T(8,128)(2,1)} %slice.531), channel_id=1, source_target_pairs={{0,1},{1,0},{2,3},{3,2},{4,5},{5,4},{6,7},{7,6},{8,9},{9,8},{10,11... | collective-permute-start | bytes 1572872 | tf_op jit(solution)/shard_map/ppermute | solution.py:276
  412.4 22.5 %collective-permute-start.54 = (bf16[256,1024]{1,0:T(8,128)(2,1)S(1)}, bf16[256,1024]{1,0:T(8,128)(2,1)}, u32[]{:S(2)}, u32[]{:S(2)}) collective-permute-start(bf16[256,1024]{1,0:T(8,128)(2,1)S(1)} %slice.526), channel_id=1, source_target_pairs={{0,1},{1,0},{2,3},{3,2},{4,5},{5,4},{6,7},{7,6},{8,9},{9,8},{10,11... | collective-permute-start | bytes 1572872 | tf_op jit(solution)/shard_map/ppermute | solution.py:276
  424.0 43.9 %collective-permute-start.52 = (bf16[256,1024]{1,0:T(8,128)(2,1)}, bf16[256,1024]{1,0:T(8,128)(2,1)}, u32[]{:S(2)}, u32[]{:S(2)}) collective-permute-start(bf16[256,1024]{1,0:T(8,128)(2,1)} %slice.527), channel_id=1, source_target_pairs={{0,1},{1,0},{2,3},{3,2},{4,5},{5,4},{6,7},{7,6},{8,9},{9,8},{10,11... | collective-permute-start | bytes 1572872 | tf_op jit(solution)/shard_map/ppermute | solution.py:276
  433.4 34.5 %collective-permute-start.41 = (bf16[256,1024]{1,0:T(8,128)(2,1)}, bf16[256,1024]{1,0:T(8,128)(2,1)}, u32[]{:S(2)}, u32[]{:S(2)}) collective-permute-start(bf16[256,1024]{1,0:T(8,128)(2,1)} %fusion.80), channel_id=1, source_target_pairs={{0,2},{1,3},{2,0},{3,1},{4,6},{5,7},{6,4},{7,5},{8,10},{9,11},{10,... | collective-permute-start | bytes 1572872 | tf_op jit(solution)/shard_map/ppermute | solution.py:276
  437.0 31.0 %collective-permute-start.55 = (bf16[256,1024]{1,0:T(8,128)(2,1)}, bf16[256,1024]{1,0:T(8,128)(2,1)}, u32[]{:S(2)}, u32[]{:S(2)}) collective-permute-start(bf16[256,1024]{1,0:T(8,128)(2,1)} %fusion.76), channel_id=1, source_target_pairs={{0,2},{1,3},{2,0},{3,1},{4,6},{5,7},{6,4},{7,5},{8,10},{9,11},{10,... | collective-permute-start | bytes 1572872 | tf_op jit(solution)/shard_map/ppermute | solution.py:276
  460.9 5.2 collective-permute-start.57
  510.6 15.4 %collective-permute-start.59 = (bf16[256,1024]{1,0:T(8,128)(2,1)}, bf16[256,1024]{1,0:T(8,128)(2,1)}, u32[]{:S(2)}, u32[]{:S(2)}) collective-permute-start(bf16[256,1024]{1,0:T(8,128)(2,1)} %reduce-scatter.11.cloned.1.call-done), channel_id=1, source_target_pairs={{0,4},{4,0},{1,5},{5,1},{2,6},{6,2},{3,7},{7,3},{8,12},{12,8},{9,1... | collective-permute-start | bytes 1572872 | tf_op jit(solution)/shard_map/ppermute | solution.py:276
  516.5 20.6 %collective-permute-start.58 = (bf16[256,1024]{1,0:T(8,128)(2,1)}, bf16[256,1024]{1,0:T(8,128)(2,1)S(1)}, u32[]{:S(2)}, u32[]{:S(2)}) collective-permute-start(bf16[256,1024]{1,0:T(8,128)(2,1)} %reduce-scatter.9.cloned.1.call-done), channel_id=1, source_target_pairs={{0,4},{4,0},{1,5},{5,1},{2,6},{6,2},{3,7},{7,3},{8,12},{12,8},{9,1... | collective-permute-start | bytes 1572872 | tf_op jit(solution)/shard_map/ppermute | solution.py:276
  520.3 23.2 %collective-permute-start.56 = (bf16[256,768]{0,1:T(8,128)(2,1)}, bf16[256,768]{0,1:T(8,128)(2,1)S(1)}, u32[]{:S(2)}, u32[]{:S(2)}) collective-permute-start(bf16[256,768]{0,1:T(8,128)(2,1)} %reduce-scatter.5.cloned.1.call-done), channel_id=1, source_target_pairs={{0,4},{4,0},{1,5},{5,1},{2,6},{6,2},{3,7},{7,3},{8,12},{12,8},{9,1... | collective-permute-start | bytes 1179656 | tf_op jit(solution)/shard_map/ppermute | solution.py:276
  (103 other events, 1002.6 us)
Sparse Core Ops, SparseCore 0:
  10.1 40.7 all-gather.5
  52.5 52.7 all-gather.7
  158.0 48.9 all-gather.9
  327.1 20.0 reduce-scatter.6
  349.3 41.8 reduce-scatter.10
  393.3 42.8 reduce-scatter.8
  461.0 33.0 reduce-scatter.4
